TPU v7x, 128 devices: a whole 4x4x4 slice. The times are simulated.
128 devices in a mesh: orb: 64 (over y, x, z), pair: 2 (over core).
Axes of the slice: x: 4, y: 4, z: 4, core: 2. Of those that a mesh axis runs over, the one named last changes fastest.
Arguments:
- wavefunctions: float32 [128, 64, 4096], P(('orb', 'pair')), may hold values from -6 to 6
- potential: float32 [64, 4096], replicated, may hold values from -1.5 to 0.5
- line_runs: int32 [2, 4096], replicated, may hold values from 0 to 64, as said below
Outputs:
- gradient: float32 [128, 64, 4096], P(('orb', 'pair'))
- preconditioned: float32 [128, 64, 4096], P(('orb', 'pair'))
Inputs may be any that keep to these rules, and one draw needn't show every extreme that they name: `line_runs`: exactly 3072 lines have start < end (runs of 1 to 32 points, start below 32); every other line has start = end = 0. The runs hold exactly 50688 grid points in all.
All inputs are finite; a program needn't handle non-finite values.
Results may differ from a plain program's by a relative error of at most 0.0001.
Values sent between devices are 32-bit elements; how exact they have to be, the bound alone decides.
A program may use at most 64 MiB of HBM per device.

v0:
```python
import math

import jax
import jax.numpy as jnp
import numpy as np
from jax import lax
from jax.experimental import pallas as pl
from jax.experimental.pallas import tpu as pltpu
from jax.sharding import PartitionSpec as P

GRID = 64
CHEB = 6
CELLS = GRID * GRID * GRID
PLANES = GRID // 2
DEVICES = 128
MESH_IDS = pl.DeviceIdType.MESH
KINETIC_SCALE = 0.125
SHIFT_VALUE = 0.25
VMEM_LIMIT = 56 * 1024 * 1024
BF16 = jnp.bfloat16
F32 = jnp.float32


def kinetic_taps():
    radius = 14
    values = np.zeros(2 * radius + 1)
    factor = float(math.factorial(radius)) ** 2
    for offset in range(1, radius + 1):
        weight = (
            2.0
            * (-1.0) ** (offset + 1)
            * factor
            / (
                offset
                * offset
                * float(math.factorial(radius - offset))
                * float(math.factorial(radius + offset))
            )
        )
        values[radius + offset] = weight
        values[radius - offset] = weight
    values[radius] = -2.0 * sum((1.0 / float(offset * offset) for offset in range(1, radius + 1)))
    return values


def magic_taps():
    shifted = np.arange(-7, 9) - 0.25
    sinc_values = np.sin(np.pi * shifted) / (np.pi * shifted)
    values = sinc_values * (0.5 + 0.5 * np.cos(np.pi * shifted / 8.5))
    return values / values.sum()


def circulant(values, first, length):
    matrix = np.zeros((length, length))
    for target in range(length):
        for position in range(values.shape[0]):
            matrix[target, (target + first + position) % length] += values[position]
    return matrix


def kinetic_spectrum():
    taps = -KINETIC_SCALE * kinetic_taps()
    offsets = np.arange(-14, 15)
    modes = np.arange(GRID).reshape(GRID, 1)
    return np.cos(2.0 * np.pi * modes * offsets.reshape(1, -1) / GRID) @ taps


def hartley():
    angle = 2.0 * np.pi * np.outer(np.arange(GRID), np.arange(GRID)) / GRID
    return (np.cos(angle) + np.sin(angle)) / np.sqrt(GRID)


def chebyshev_symbol():
    line = kinetic_spectrum()
    low_end = SHIFT_VALUE
    high_end = SHIFT_VALUE + 3.0 * float(line.max())
    centre_value = 0.5 * (high_end + low_end)
    half_width = 0.5 * (high_end - low_end)
    ratio_base = centre_value / half_width
    rho_value = 1.0 / ratio_base
    operator = line[:, None, None] + line[None, :, None] + line[None, None, :] + SHIFT_VALUE
    solution_value = np.zeros_like(operator)
    residual = np.ones_like(operator)
    direction = residual / centre_value
    for counter in range(CHEB):
        solution_value = solution_value + direction
        if counter + 1 < CHEB:
            residual = residual - operator * direction
            rho_next = 1.0 / (2.0 * ratio_base - rho_value)
            direction = rho_next * rho_value * direction + 2.0 * rho_next / half_width * residual
            rho_value = rho_next
    return solution_value.reshape(GRID * PLANES, 128).astype(np.float32)


def split_table(matrix):
    high = np.asarray(matrix, np.float32).astype(jnp.bfloat16)
    low = (np.asarray(matrix, np.float64) - high.astype(np.float64)).astype(np.float32).astype(jnp.bfloat16)
    return high, low


def rows_table(matrix):
    high, low = split_table(matrix)
    return np.concatenate([high, high, low], axis=1)


def lanes_table(*matrices):
    wide = np.concatenate([np.kron(np.eye(2), matrix.T) for matrix in matrices], axis=1)
    high, low = split_table(wide)
    return np.concatenate([high, high, low], axis=0)


def planes_table(matrix):
    even = np.concatenate([matrix[0::2, 0::2], matrix[0::2, 1::2]], axis=1)
    odd = np.concatenate([matrix[1::2, 1::2], matrix[1::2, 0::2]], axis=1)
    return rows_table(np.concatenate([even, odd], axis=0))


def split_pair(value):
    high = value.astype(BF16)
    low = (value - high.astype(F32)).astype(BF16)
    return high, low


def dot32(left, right):
    return jnp.dot(left, right, preferred_element_type=F32)


def along_rows(table, value):
    high, low = split_pair(value)
    return dot32(table, jnp.concatenate([high, low, high], axis=0))


def along_lanes(table, value):
    high, low = split_pair(value)
    return dot32(jnp.concatenate([high, low], axis=1), table[:256]) + dot32(high, table[256:])


def lane_index(shape):
    return lax.broadcasted_iota(jnp.int32, shape, 1)


def plane_stack(value):
    swapped = jnp.concatenate(
        [pltpu.roll(value[:, :128], 64, 1), pltpu.roll(value[:, 128:], 64, 1)], axis=1
    )
    high, low = split_pair(jnp.concatenate([value, swapped], axis=0))
    return jnp.concatenate([high, low, high], axis=0)


def plane_pick(product):
    half = lane_index((PLANES, 256)) % 128 < 64
    return jnp.where(half, product[:PLANES], product[PLANES:])


def two_planes(ref, first):
    return jnp.concatenate(
        [ref[pl.ds(first, PLANES, stride=GRID), :], ref[pl.ds(first + 1, PLANES, stride=GRID), :]],
        axis=1,
    )


def put_two_planes(ref, first, value):
    ref[pl.ds(first, PLANES, stride=GRID), :] = value[:, :128]
    ref[pl.ds(first + 1, PLANES, stride=GRID), :] = value[:, 128:]


def block_of(plane):
    return pl.ds(pl.multiple_of(plane * GRID, GRID), GRID)


def run_bounds(runs):
    row = lax.broadcasted_iota(jnp.int32, (GRID, PLANES), 0)
    column = lax.broadcasted_iota(jnp.int32, (GRID, PLANES), 1)
    repeat = (row // 2 == column).astype(F32).astype(BF16)
    own = lax.broadcasted_iota(jnp.int32, (GRID, 128), 0) % 2 == lane_index((GRID, 128)) // 64
    bounds = []
    for bound in range(2):
        lines = runs[bound : bound + 1, :].reshape(PLANES, 128).astype(F32).astype(BF16)
        bounds.append(jnp.where(own, dot32(repeat, lines), 0.0))
    return jnp.concatenate(bounds, axis=0).astype(BF16)


def region_pair(bounds, pair):
    lane = lane_index((128, 256))
    line = lax.broadcasted_iota(jnp.int32, (128, 256), 0) % GRID
    pick = (line == lane // 64 + 4 * pair).astype(F32).astype(BF16)
    spread = dot32(bounds, pick)
    depth = (lane_index((GRID, 256)) % GRID).astype(F32)
    return ((depth >= spread[:GRID]) & (depth < spread[GRID:])).astype(F32)


def fold_pair(value):
    first, second = value[:, :128], value[:, 128:]
    lower = (lane_index((GRID, 128)) // 32) % 2 == 0
    return jnp.where(lower, first + pltpu.roll(first, 96, 1), second + pltpu.roll(second, 32, 1))


def unfold_pair(tile):
    lower = (lane_index((GRID, 128)) // 32) % 2 == 0
    first = jnp.where(lower, tile, pltpu.roll(tile, 32, 1))
    second = jnp.where(lower, pltpu.roll(tile, 96, 1), tile)
    return jnp.concatenate([first, second], axis=1)


def load_planes(hbm, vmem, sem):
    for plane in range(PLANES):
        pltpu.make_async_copy(
            hbm.at[:, pl.ds(plane * 128, 128)], vmem.at[pl.ds(plane * GRID, GRID), :], sem
        ).start()


def wait_planes(vmem, sem):
    pltpu.make_async_copy(vmem, vmem, sem).wait()


def both_planes(ref, pair):
    return jnp.concatenate([ref[block_of(2 * pair), :], ref[block_of(2 * pair + 1), :]], axis=1)


def put_both_planes(ref, pair, value):
    ref[block_of(2 * pair), :] = value[:, :128]
    ref[block_of(2 * pair + 1), :] = value[:, 128:]


def lanes_pair(table, value):
    stacked = along_lanes(table, jnp.concatenate([value[:, :128], value[:, 128:]], axis=0))
    return stacked[:GRID], stacked[GRID:]


HALF_LOOP = 16


def hamiltonian_head(masked, kinetic, forward, tables, pair, value):
    lanes_kf, rows_k, rows_f = tables
    first, second = lanes_pair(lanes_kf[...], value)
    put_both_planes(masked, pair, value)
    along = jnp.concatenate([first[:, :128], second[:, :128]], axis=1) + along_rows(rows_k[...], value)
    put_both_planes(kinetic, pair, along)
    magic = jnp.concatenate([first[:, 128:], second[:, 128:]], axis=1)
    put_both_planes(forward, pair, along_rows(rows_f[...], magic))


def hamiltonian_middle(masked, kinetic, forward, potential, tables, step):
    planes_k, planes_f, planes_b = tables
    first = 2 * step
    real = plane_pick(dot32(planes_f[...], plane_stack(two_planes(forward, first))))
    weighted = real * two_planes(potential, first)
    put_two_planes(forward, first, plane_pick(dot32(planes_b[...], plane_stack(weighted))))
    along = plane_pick(dot32(planes_k[...], plane_stack(two_planes(masked, first))))
    put_two_planes(kinetic, first, two_planes(kinetic, first) + along)


def hamiltonian_tail(kinetic, forward, tables, pair):
    rows_b, lanes_b = tables
    first, second = lanes_pair(lanes_b[...], along_rows(rows_b[...], both_planes(forward, pair)))
    return both_planes(kinetic, pair) + jnp.concatenate([first, second], axis=1)


def loop(count, body, unroll=1):
    def step(index, carry):
        body(index)
        return carry

    lax.fori_loop(0, count, step, 0, unroll=unroll)


def precondition_kernel(
    tiles, runs, lanes_q, rows_q, planes_q, symbol_hbm, gradient_out, preconditioned_out,
    region, gradient, work, symbol, sems,
):
    fetch = pltpu.make_async_copy(symbol_hbm, symbol, sems.at[0])
    fetch.start()
    bounds = run_bounds(runs[...])

    def put(buffer, target, plane, sem):
        return pltpu.make_async_copy(
            buffer.at[block_of(plane), :],
            target.at[0, :, pl.ds(pl.multiple_of(plane * 128, 128), 128)],
            sem,
        )

    def head(pair):
        mask = region_pair(bounds, pair)
        put_both_planes(region, pair, mask)
        value = unfold_pair(tiles[block_of(pair), :]) * mask
        put_both_planes(gradient, pair, value)
        put(gradient, gradient_out, 2 * pair, sems.at[1]).start()
        put(gradient, gradient_out, 2 * pair + 1, sems.at[1]).start()
        first, second = lanes_pair(lanes_q[...], value)
        put_both_planes(work, pair, along_rows(rows_q[...], jnp.concatenate([first, second], axis=1)))

    loop(PLANES // 2, head, HEAD_UNROLL)
    fetch.wait()

    def middle(step):
        first = 2 * step
        modes = plane_pick(dot32(planes_q[...], plane_stack(two_planes(work, first))))
        factor = jnp.concatenate([symbol[pl.ds(pl.multiple_of(first * PLANES, 64), PLANES), :],
                                  symbol[pl.ds(pl.multiple_of(first * PLANES, 64) + PLANES, PLANES), :]], axis=1)
        put_two_planes(work, first, plane_pick(dot32(planes_q[...], plane_stack(modes * factor))))

    loop(GRID // 2, middle, MIDDLE_UNROLL)
    wait_planes(gradient, sems.at[1])

    def tail(pair):
        first, second = lanes_pair(lanes_q[...], along_rows(rows_q[...], both_planes(work, pair)))
        value = jnp.concatenate([first, second], axis=1) * both_planes(region, pair)
        put_both_planes(work, pair, value)
        put(work, preconditioned_out, 2 * pair, sems.at[2]).start()
        put(work, preconditioned_out, 2 * pair + 1, sems.at[2]).start()

    loop(PLANES // 2, tail, HEAD_UNROLL)
    wait_planes(work, sems.at[2])


HEAD_UNROLL = 4
MIDDLE_UNROLL = 4


def in_vmem(count):
    return [pl.BlockSpec(memory_space=pltpu.VMEM)] * count


def precondition(tiles, line_runs):
    modes = hartley()
    field = pltpu.VMEM((GRID * PLANES, 128), F32)
    shape = jax.ShapeDtypeStruct((1, GRID, GRID * GRID), F32)
    return pl.pallas_call(
        precondition_kernel,
        out_shape=(shape, shape),
        in_specs=in_vmem(5) + [pl.BlockSpec(memory_space=pl.ANY)],
        out_specs=[pl.BlockSpec(memory_space=pl.ANY)] * 2,
        scratch_shapes=[field, field, field, field, pltpu.SemaphoreType.DMA((3,))],
        compiler_params=pltpu.CompilerParams(vmem_limit_bytes=VMEM_LIMIT),
        name="precondition",
    )(
        tiles,
        line_runs,
        jnp.asarray(lanes_table(modes)),
        jnp.asarray(rows_table(modes)),
        jnp.asarray(planes_table(modes)),
        jnp.asarray(chebyshev_symbol()),
    )


def apply_kernel(
    wave, potential_hbm, runs, lanes_kf, rows_k, rows_f, planes_k, planes_f, planes_b, rows_b, lanes_b,
    masked_tiles, applied_tiles,
    region, masked, kinetic, forward, potential, sems,
):
    load_planes(wave.at[0], masked, sems.at[0])
    load_planes(potential_hbm, potential, sems.at[1])
    bounds = run_bounds(runs[...])
    wait_planes(masked, sems.at[0])

    def head(pair):
        mask = region_pair(bounds, pair)
        put_both_planes(region, pair, mask)
        value = both_planes(masked, pair) * mask
        masked_tiles[block_of(pair), :] = fold_pair(value)
        hamiltonian_head(masked, kinetic, forward, (lanes_kf, rows_k, rows_f), pair, value)

    loop(PLANES // 2, head, HEAD_UNROLL)
    wait_planes(potential, sems.at[1])
    loop(
        GRID // 2,
        lambda step: hamiltonian_middle(
            masked, kinetic, forward, potential, (planes_k, planes_f, planes_b), step
        ),
        MIDDLE_UNROLL,
    )

    def tail(pair):
        value = hamiltonian_tail(kinetic, forward, (rows_b, lanes_b), pair) * both_planes(region, pair)
        applied_tiles[block_of(pair), :] = fold_pair(value)

    loop(PLANES // 2, tail, HEAD_UNROLL)


def hamiltonian_tables():
    kinetic = -KINETIC_SCALE * circulant(kinetic_taps(), -14, GRID)
    magic = circulant(magic_taps(), -7, GRID)
    tables = (
        lanes_table(kinetic, magic),
        rows_table(kinetic),
        rows_table(magic),
        planes_table(kinetic),
        planes_table(magic),
        planes_table(magic.T),
        rows_table(magic.T),
        lanes_table(magic.T),
    )
    return [jnp.asarray(table) for table in tables]


def apply_fields(wavefunctions, potential, line_runs):
    field = pltpu.VMEM((GRID * PLANES, 128), F32)
    tiles = jax.ShapeDtypeStruct((8 * DEVICES, 128), F32)
    anywhere = [pl.BlockSpec(memory_space=pl.ANY)]
    return pl.pallas_call(
        apply_kernel,
        out_shape=(tiles, tiles),
        in_specs=anywhere * 2 + in_vmem(9),
        out_specs=in_vmem(2),
        scratch_shapes=[field, field, field, field, field, pltpu.SemaphoreType.DMA((2,))],
        compiler_params=pltpu.CompilerParams(vmem_limit_bytes=VMEM_LIMIT),
        name="apply",
    )(wavefunctions, potential, line_runs, *hamiltonian_tables())


def tile_of(index):
    return pl.ds(pl.multiple_of(index * 8, 8), 8)


def peer_id(index):
    return (index // 2, lax.rem(index, 2))


def exchange_kernel(
    masked_send, applied_send, gradient_out,
    masked_recv, applied_recv, back_send, partial, gathered, row, matrix,
    send_sems, recv_sems,
):
    me = lax.axis_index("orb") * 2 + lax.axis_index("pair")
    barrier = pltpu.get_barrier_semaphore()

    def peer_at(step):
        return lax.rem(me + step, DEVICES)

    def greet(step, carry):
        pl.semaphore_signal(barrier, inc=1, device_id=peer_id(peer_at(step)), device_id_type=MESH_IDS)
        return carry

    lax.fori_loop(1, DEVICES, greet, 0)
    pl.semaphore_wait(barrier, DEVICES - 1)

    def scatter(source, target, phase, source_at, target_at):
        def send(step, carry):
            peer = peer_at(step)
            pltpu.make_async_remote_copy(
                src_ref=source.at[source_at(peer)],
                dst_ref=target.at[target_at(me)],
                send_sem=send_sems.at[phase],
                recv_sem=recv_sems.at[phase],
                device_id=peer_id(peer),
                device_id_type=MESH_IDS,
            ).start()
            return carry

        lax.fori_loop(1, DEVICES, send, 0)

    def drain(buffer, sem):
        whole = buffer.at[pl.ds(0, buffer.shape[0] * (DEVICES - 1) // DEVICES)]
        pltpu.make_async_copy(whole, whole, sem).wait()

    def row_of(index):
        return pl.ds(index, 1)

    scatter(masked_send, masked_recv, 0, tile_of, tile_of)
    scatter(applied_send, applied_recv, 1, tile_of, tile_of)
    masked_recv[tile_of(me), :] = masked_send[tile_of(me), :]
    applied_recv[tile_of(me), :] = applied_send[tile_of(me), :]
    drain(masked_recv, recv_sems.at[0])
    drain(applied_recv, recv_sems.at[1])

    total = jnp.zeros((DEVICES, DEVICES), jnp.float32)
    for sub in range(8):
        masked_high, masked_low = split_pair(masked_recv[pl.ds(sub, DEVICES, stride=8), :])
        applied_high, applied_low = split_pair(applied_recv[pl.ds(sub, DEVICES, stride=8), :])
        for left, right in ((applied_high, masked_high), (applied_high, masked_low), (applied_low, masked_high)):
            total = total + lax.dot_general(
                left, right, (((1,), (1,)), ((), ())), preferred_element_type=jnp.float32
            )
    partial[:, 0, :] = total
    scatter(partial, gathered, 2, row_of, row_of)
    gathered[row_of(me)] = partial[row_of(me)]
    drain(gathered, recv_sems.at[2])
    row[...] = jnp.sum(gathered[...], axis=0, keepdims=True) * (1.0 / (GRID * GRID * GRID))
    scatter(row, matrix, 3, lambda peer: pl.ds(0, 1), row_of)
    matrix[row_of(me)] = row[...]
    drain(matrix, recv_sems.at[3])
    matrix_high, matrix_low = split_pair(matrix[:, 0, :])
    for sub in range(8):
        rows = pl.ds(sub, DEVICES, stride=8)
        masked_high, masked_low = split_pair(masked_recv[rows, :])
        projected = jnp.dot(matrix_high, masked_high, preferred_element_type=jnp.float32)
        projected = projected + jnp.dot(matrix_high, masked_low, preferred_element_type=jnp.float32)
        projected = projected + jnp.dot(matrix_low, masked_high, preferred_element_type=jnp.float32)
        back_send[rows, :] = applied_recv[rows, :] - projected
    scatter(back_send, gradient_out, 4, tile_of, tile_of)
    gradient_out[tile_of(me), :] = back_send[tile_of(me), :]
    drain(gradient_out, recv_sems.at[4])
    drain(masked_send, send_sems.at[0])
    drain(applied_send, send_sems.at[1])
    drain(partial, send_sems.at[2])
    drain(matrix, send_sems.at[3])
    drain(back_send, send_sems.at[4])


def exchange(masked_tiles, applied_tiles):
    tiles = (8 * DEVICES, 128)
    return pl.pallas_call(
        exchange_kernel,
        out_shape=jax.ShapeDtypeStruct(tiles, jnp.float32),
        in_specs=[pl.BlockSpec(memory_space=pltpu.VMEM)] * 2,
        out_specs=pl.BlockSpec(memory_space=pltpu.VMEM),
        scratch_shapes=[
            pltpu.VMEM(tiles, jnp.float32),
            pltpu.VMEM(tiles, jnp.float32),
            pltpu.VMEM(tiles, jnp.float32),
            pltpu.VMEM((DEVICES, 1, 128), jnp.float32),
            pltpu.VMEM((DEVICES, 1, 128), jnp.float32),
            pltpu.VMEM((1, 1, 128), jnp.float32),
            pltpu.VMEM((DEVICES, 1, 128), jnp.float32),
            pltpu.SemaphoreType.DMA((5,)),
            pltpu.SemaphoreType.DMA((5,)),
        ],
        compiler_params=pltpu.CompilerParams(collective_id=0, has_side_effects=True),
        name="exchange",
    )(masked_tiles, applied_tiles)


def on_device(wavefunctions, potential, line_runs):
    masked_tiles, applied_tiles = apply_fields(wavefunctions, potential, line_runs)
    tiles = exchange(masked_tiles, applied_tiles)
    return precondition(tiles, line_runs)


def solution(mesh):
    return jax.shard_map(
        on_device,
        mesh=mesh,
        in_specs=(P(("orb", "pair"), None, None), P(), P()),
        out_specs=(P(("orb", "pair"), None, None), P(("orb", "pair"), None, None)),
        check_vma=False,
    )
```

profile of v0, /device:TPU:0, one launch (start us, length us, event | category | flops | bytes accessed | tf_op | source)
XLA Modules:
  0.0 90.9 jit_solution(1843646271927769733)
XLA Ops:
  0.6 20.6 %apply.1 = (f32[1024,128]{1,0:T(8,128)}, f32[1024,128]{1,0:T(8,128)}) custom-call(f32[1,64,4096]{2,1,0:T(8,128)} %wave.1, f32[64,4096]{1,0:T(8,128)} %potential_hbm.1, s32[2,4096]{1,0:T(2,128)} %runs.3, bf16[384,256]{1,0:T(8,128)(2,1)} %constant.24.clone.lanes_kf, bf16[64,192]{1,0:T(8,128)(2,1)} %constant.25.clone.rows_k, ...), custom_call_target="tpu_custom_call" | custom-call | tf_op jit(solution)/shard_map/apply/pallas_call | solution.py:400
  21.2 54.7 %exchange.1.tiles = f32[1024,128]{1,0:T(8,128)} custom-call(f32[1024,128]{1,0:T(8,128)} %get-tuple-element.4.masked_send, f32[1024,128]{1,0:T(8,128)} %get-tuple-element.5.applied_send), custom_call_target="tpu_custom_call" | custom-call | tf_op jit(solution)/shard_map/exchange/pallas_call | solution.py:502
  75.9 15.0 %precondition.1 = (f32[1,64,4096]{2,1,0:T(8,128)}, f32[1,64,4096]{2,1,0:T(8,128)}) custom-call(f32[1024,128]{1,0:T(8,128)} %exchange.1.tiles, s32[2,4096]{1,0:T(2,128)} %runs.3, bf16[384,128]{1,0:T(8,128)(2,1)} %constant.32.clone.lanes_q, bf16[64,192]{1,0:T(8,128)(2,1)} %constant.33.clone.rows_q, bf16[64,192]{1,0:T(8,128)(2,1)} %constant.34.clone.planes_q, ...), custom_call_target="tpu_custom_call" | custom-call | tf_op jit(solution)/shard_map/precondition/pallas_call | solution.py:328
where the time goes:
time: 91.9 us; the launch traced here: 90.9 us
  Pallas kernels  90.3 us (98%)
    pallas_call x1, Pallas kernels, exchange(): pl.pallas_call(exchange_kernel, out_shape=jax.ShapeDtypeStruct(tiles, jnp...  54.7 us
    pallas_call x1, Pallas kernels, apply_fields(): pl.pallas_call(apply_kernel, out_shape=(tiles, tiles), in_specs=anywhere...  20.6 us
    pallas_call x1, Pallas kernels, precondition(): pl.pallas_call(precondition_kernel, out_shape=(shape, shape), in_specs=in...  15 us

commit v1 on v0

--- a/solution.py
+++ b/solution.py
@@ -343,40 +343,6 @@
     )
 
 
-def apply_kernel(
-    wave, potential_hbm, runs, lanes_kf, rows_k, rows_f, planes_k, planes_f, planes_b, rows_b, lanes_b,
-    masked_tiles, applied_tiles,
-    region, masked, kinetic, forward, potential, sems,
-):
-    load_planes(wave.at[0], masked, sems.at[0])
-    load_planes(potential_hbm, potential, sems.at[1])
-    bounds = run_bounds(runs[...])
-    wait_planes(masked, sems.at[0])
-
-    def head(pair):
-        mask = region_pair(bounds, pair)
-        put_both_planes(region, pair, mask)
-        value = both_planes(masked, pair) * mask
-        masked_tiles[block_of(pair), :] = fold_pair(value)
-        hamiltonian_head(masked, kinetic, forward, (lanes_kf, rows_k, rows_f), pair, value)
-
-    loop(PLANES // 2, head, HEAD_UNROLL)
-    wait_planes(potential, sems.at[1])
-    loop(
-        GRID // 2,
-        lambda step: hamiltonian_middle(
-            masked, kinetic, forward, potential, (planes_k, planes_f, planes_b), step
-        ),
-        MIDDLE_UNROLL,
-    )
-
-    def tail(pair):
-        value = hamiltonian_tail(kinetic, forward, (rows_b, lanes_b), pair) * both_planes(region, pair)
-        applied_tiles[block_of(pair), :] = fold_pair(value)
-
-    loop(PLANES // 2, tail, HEAD_UNROLL)
-
-
 def hamiltonian_tables():
     kinetic = -KINETIC_SCALE * circulant(kinetic_taps(), -14, GRID)
     magic = circulant(magic_taps(), -7, GRID)
@@ -393,33 +359,25 @@
     return [jnp.asarray(table) for table in tables]
 
 
-def apply_fields(wavefunctions, potential, line_runs):
-    field = pltpu.VMEM((GRID * PLANES, 128), F32)
-    tiles = jax.ShapeDtypeStruct((8 * DEVICES, 128), F32)
-    anywhere = [pl.BlockSpec(memory_space=pl.ANY)]
-    return pl.pallas_call(
-        apply_kernel,
-        out_shape=(tiles, tiles),
-        in_specs=anywhere * 2 + in_vmem(9),
-        out_specs=in_vmem(2),
-        scratch_shapes=[field, field, field, field, field, pltpu.SemaphoreType.DMA((2,))],
-        compiler_params=pltpu.CompilerParams(vmem_limit_bytes=VMEM_LIMIT),
-        name="apply",
-    )(wavefunctions, potential, line_runs, *hamiltonian_tables())
-
-
 def tile_of(index):
     return pl.ds(pl.multiple_of(index * 8, 8), 8)
 
 
+def row_of(index):
+    return pl.ds(index, 1)
+
+
 def peer_id(index):
     return (index // 2, lax.rem(index, 2))
 
 
-def exchange_kernel(
-    masked_send, applied_send, gradient_out,
-    masked_recv, applied_recv, back_send, partial, gathered, row, matrix,
-    send_sems, recv_sems,
+def gradient_kernel(
+    wave, potential_hbm, runs, lanes_kf, rows_k, rows_f, planes_k, planes_f, planes_b, rows_b, lanes_b,
+    gradient_tiles,
+    region, masked, kinetic, forward, potential,
+    masked_send, masked_recv, applied_send, applied_recv, back_send,
+    partial, gathered, row, matrix,
+    load_sems, send_sems, recv_sems,
 ):
     me = lax.axis_index("orb") * 2 + lax.axis_index("pair")
     barrier = pltpu.get_barrier_semaphore()
@@ -427,69 +385,108 @@
     def peer_at(step):
         return lax.rem(me + step, DEVICES)
 
-    def greet(step, carry):
-        pl.semaphore_signal(barrier, inc=1, device_id=peer_id(peer_at(step)), device_id_type=MESH_IDS)
-        return carry
-
-    lax.fori_loop(1, DEVICES, greet, 0)
-    pl.semaphore_wait(barrier, DEVICES - 1)
+    def greet(step):
+        pl.semaphore_signal(
+            barrier, inc=1, device_id=peer_id(peer_at(step + 1)), device_id_type=MESH_IDS
+        )
+
+    load_planes(wave.at[0], masked, load_sems.at[0])
+    load_planes(potential_hbm, potential, load_sems.at[1])
+    loop(DEVICES - 1, greet)
+    bounds = run_bounds(runs[...])
+    wait_planes(masked, load_sems.at[0])
+
+    def send(source, target, phase, peer, source_at, target_at):
+        pltpu.make_async_remote_copy(
+            src_ref=source.at[source_at(peer)],
+            dst_ref=target.at[target_at(me)],
+            send_sem=send_sems.at[phase],
+            recv_sem=recv_sems.at[phase],
+            device_id=peer_id(peer),
+            device_id_type=MESH_IDS,
+        ).start()
 
     def scatter(source, target, phase, source_at, target_at):
-        def send(step, carry):
-            peer = peer_at(step)
-            pltpu.make_async_remote_copy(
-                src_ref=source.at[source_at(peer)],
-                dst_ref=target.at[target_at(me)],
-                send_sem=send_sems.at[phase],
-                recv_sem=recv_sems.at[phase],
-                device_id=peer_id(peer),
-                device_id_type=MESH_IDS,
-            ).start()
-            return carry
-
-        lax.fori_loop(1, DEVICES, send, 0)
+        loop(
+            DEVICES - 1,
+            lambda step: send(source, target, phase, peer_at(step + 1), source_at, target_at),
+        )
+
+    def send_tile(source, target, phase, tile):
+        @pl.when(tile != me)
+        def _():
+            send(source, target, phase, tile, tile_of, tile_of)
 
     def drain(buffer, sem):
         whole = buffer.at[pl.ds(0, buffer.shape[0] * (DEVICES - 1) // DEVICES)]
         pltpu.make_async_copy(whole, whole, sem).wait()
 
-    def row_of(index):
-        return pl.ds(index, 1)
-
-    scatter(masked_send, masked_recv, 0, tile_of, tile_of)
-    scatter(applied_send, applied_recv, 1, tile_of, tile_of)
+    def head(pair):
+        mask = region_pair(bounds, pair)
+        put_both_planes(region, pair, mask)
+        value = both_planes(masked, pair) * mask
+        masked_send[block_of(pair), :] = fold_pair(value)
+        hamiltonian_head(masked, kinetic, forward, (lanes_kf, rows_k, rows_f), pair, value)
+
+    loop(PLANES // 2, head, HEAD_UNROLL)
+    wait_planes(potential, load_sems.at[1])
+    pl.semaphore_wait(barrier, DEVICES - 1)
+
+    def middle(step):
+        for sub in range(4):
+            send_tile(masked_send, masked_recv, 0, peer_at(4 * step + sub))
+        hamiltonian_middle(
+            masked, kinetic, forward, potential, (planes_k, planes_f, planes_b), step
+        )
+
+    loop(GRID // 2, middle, MIDDLE_UNROLL)
     masked_recv[tile_of(me), :] = masked_send[tile_of(me), :]
+
+    def tail(step):
+        pair = lax.rem(step + me // 8, PLANES // 2)
+        value = hamiltonian_tail(kinetic, forward, (rows_b, lanes_b), pair) * both_planes(region, pair)
+        applied_send[block_of(pair), :] = fold_pair(value)
+        for sub in range(8):
+            send_tile(applied_send, applied_recv, 1, 8 * pair + lax.rem(me + sub, 8))
+
+    loop(PLANES // 2, tail, TAIL_UNROLL)
     applied_recv[tile_of(me), :] = applied_send[tile_of(me), :]
     drain(masked_recv, recv_sems.at[0])
     drain(applied_recv, recv_sems.at[1])
 
-    total = jnp.zeros((DEVICES, DEVICES), jnp.float32)
+    total = jnp.zeros((DEVICES, DEVICES), F32)
     for sub in range(8):
-        masked_high, masked_low = split_pair(masked_recv[pl.ds(sub, DEVICES, stride=8), :])
-        applied_high, applied_low = split_pair(applied_recv[pl.ds(sub, DEVICES, stride=8), :])
-        for left, right in ((applied_high, masked_high), (applied_high, masked_low), (applied_low, masked_high)):
-            total = total + lax.dot_general(
-                left, right, (((1,), (1,)), ((), ())), preferred_element_type=jnp.float32
-            )
+        rows = pl.ds(sub, DEVICES, stride=8)
+        masked_high, masked_low = split_pair(masked_recv[rows, :])
+        applied_high, applied_low = split_pair(applied_recv[rows, :])
+        total = total + lax.dot_general(
+            jnp.concatenate([applied_high, applied_low], axis=1),
+            jnp.concatenate([masked_high, masked_high], axis=1),
+            (((1,), (1,)), ((), ())),
+            preferred_element_type=F32,
+        )
+        total = total + lax.dot_general(
+            applied_high, masked_low, (((1,), (1,)), ((), ())), preferred_element_type=F32
+        )
     partial[:, 0, :] = total
     scatter(partial, gathered, 2, row_of, row_of)
     gathered[row_of(me)] = partial[row_of(me)]
     drain(gathered, recv_sems.at[2])
-    row[...] = jnp.sum(gathered[...], axis=0, keepdims=True) * (1.0 / (GRID * GRID * GRID))
+    row[...] = jnp.sum(gathered[...], axis=0, keepdims=True) * (1.0 / CELLS)
     scatter(row, matrix, 3, lambda peer: pl.ds(0, 1), row_of)
     matrix[row_of(me)] = row[...]
     drain(matrix, recv_sems.at[3])
     matrix_high, matrix_low = split_pair(matrix[:, 0, :])
+    table = jnp.concatenate([matrix_high, matrix_low], axis=1)
     for sub in range(8):
         rows = pl.ds(sub, DEVICES, stride=8)
         masked_high, masked_low = split_pair(masked_recv[rows, :])
-        projected = jnp.dot(matrix_high, masked_high, preferred_element_type=jnp.float32)
-        projected = projected + jnp.dot(matrix_high, masked_low, preferred_element_type=jnp.float32)
-        projected = projected + jnp.dot(matrix_low, masked_high, preferred_element_type=jnp.float32)
+        projected = dot32(table, jnp.concatenate([masked_high, masked_high], axis=0))
+        projected = projected + dot32(matrix_high, masked_low)
         back_send[rows, :] = applied_recv[rows, :] - projected
-    scatter(back_send, gradient_out, 4, tile_of, tile_of)
-    gradient_out[tile_of(me), :] = back_send[tile_of(me), :]
-    drain(gradient_out, recv_sems.at[4])
+    scatter(back_send, gradient_tiles, 4, tile_of, tile_of)
+    gradient_tiles[tile_of(me), :] = back_send[tile_of(me), :]
+    drain(gradient_tiles, recv_sems.at[4])
     drain(masked_send, send_sems.at[0])
     drain(applied_send, send_sems.at[1])
     drain(partial, send_sems.at[2])
@@ -497,32 +494,35 @@
     drain(back_send, send_sems.at[4])
 
 
-def exchange(masked_tiles, applied_tiles):
-    tiles = (8 * DEVICES, 128)
+TAIL_UNROLL = 1
+
+
+def gradient_fields(wavefunctions, potential, line_runs):
+    field = pltpu.VMEM((GRID * PLANES, 128), F32)
+    tiles = pltpu.VMEM((8 * DEVICES, 128), F32)
+    rows = pltpu.VMEM((DEVICES, 1, 128), F32)
     return pl.pallas_call(
-        exchange_kernel,
-        out_shape=jax.ShapeDtypeStruct(tiles, jnp.float32),
-        in_specs=[pl.BlockSpec(memory_space=pltpu.VMEM)] * 2,
+        gradient_kernel,
+        out_shape=jax.ShapeDtypeStruct((8 * DEVICES, 128), F32),
+        in_specs=[pl.BlockSpec(memory_space=pl.ANY)] * 2 + in_vmem(9),
         out_specs=pl.BlockSpec(memory_space=pltpu.VMEM),
         scratch_shapes=[
-            pltpu.VMEM(tiles, jnp.float32),
-            pltpu.VMEM(tiles, jnp.float32),
-            pltpu.VMEM(tiles, jnp.float32),
-            pltpu.VMEM((DEVICES, 1, 128), jnp.float32),
-            pltpu.VMEM((DEVICES, 1, 128), jnp.float32),
-            pltpu.VMEM((1, 1, 128), jnp.float32),
-            pltpu.VMEM((DEVICES, 1, 128), jnp.float32),
+            field, field, field, field, field,
+            tiles, tiles, tiles, tiles, tiles,
+            rows, rows, pltpu.VMEM((1, 1, 128), F32), rows,
+            pltpu.SemaphoreType.DMA((2,)),
             pltpu.SemaphoreType.DMA((5,)),
             pltpu.SemaphoreType.DMA((5,)),
         ],
-        compiler_params=pltpu.CompilerParams(collective_id=0, has_side_effects=True),
-        name="exchange",
-    )(masked_tiles, applied_tiles)
+        compiler_params=pltpu.CompilerParams(
+            collective_id=0, has_side_effects=True, vmem_limit_bytes=VMEM_LIMIT
+        ),
+        name="gradient",
+    )(wavefunctions, potential, line_runs, *hamiltonian_tables())
 
 
 def on_device(wavefunctions, potential, line_runs):
-    masked_tiles, applied_tiles = apply_fields(wavefunctions, potential, line_runs)
-    tiles = exchange(masked_tiles, applied_tiles)
+    tiles = gradient_fields(wavefunctions, potential, line_runs)
     return precondition(tiles, line_runs)
 
 

time: 91.9 us -> 84.6 us (0.921)
  Pallas kernels: 90.3 us -> 83 us
    pallas_call x2 -> x1, Pallas kernels: 75.3 us -> 68.1 us  [gradient_fields(): pl.pallas_call(gradient_kernel, out_shape=jax.ShapeDtypeStruct((8 * DEVIC...]
where the time goes in v1:
time: 84.6 us; the launch traced here: 83.7 us
  Pallas kernels  83 us (98%)
    pallas_call x1, Pallas kernels, gradient_fields(): pl.pallas_call(gradient_kernel, out_shape=jax.ShapeDtypeStruct((8 * DEVIC...  68.1 us
    pallas_call x1, Pallas kernels, precondition(): pl.pallas_call(precondition_kernel, out_shape=(shape, shape), in_specs=in...  15 us

profile of v1, /device:TPU:0, one launch (start us, length us, event | category | flops | bytes accessed | tf_op | source)
XLA Modules:
  0.0 83.7 jit_solution(9318593986527143267)
XLA Ops:
  0.6 68.1 %gradient.1.tiles = f32[1024,128]{1,0:T(8,128)} custom-call(f32[1,64,4096]{2,1,0:T(8,128)} %wave.1, f32[64,4096]{1,0:T(8,128)} %potential_hbm.1, s32[2,4096]{1,0:T(2,128)} %runs.3, bf16[384,256]{1,0:T(8,128)(2,1)} %constant.24.clone.lanes_kf, bf16[64,192]{1,0:T(8,128)(2,1)} %constant.25.clone.rows_k, bf16[64,192]{1,0:T(8,128)(2,1)} %constant.26.clone.rows_f, ...), custom_call_target="tpu_custom_call" | custom-call | tf_op jit(solution)/shard_map/gradient/pallas_call | solution.py:504
  68.7 15.0 %precondition.1 = (f32[1,64,4096]{2,1,0:T(8,128)}, f32[1,64,4096]{2,1,0:T(8,128)}) custom-call(f32[1024,128]{1,0:T(8,128)} %gradient.1.tiles, s32[2,4096]{1,0:T(2,128)} %runs.3, bf16[384,128]{1,0:T(8,128)(2,1)} %constant.32.clone.lanes_q, bf16[64,192]{1,0:T(8,128)(2,1)} %constant.33.clone.rows_q, bf16[64,192]{1,0:T(8,128)(2,1)} %constant.34.clone.planes_q, ...), custom_call_target="tpu_custom_call" | custom-call | tf_op jit(solution)/shard_map/precondition/pallas_call | solution.py:328

commit v2 on v1

v2 whole, which is shorter than its diff:
```python
import math

import jax
import jax.numpy as jnp
import numpy as np
from jax import lax
from jax.experimental import pallas as pl
from jax.experimental.pallas import tpu as pltpu
from jax.sharding import PartitionSpec as P

GRID = 64
CHEB = 6
CELLS = GRID * GRID * GRID
PLANES = GRID // 2
DEVICES = 128
MESH_IDS = pl.DeviceIdType.MESH
KINETIC_SCALE = 0.125
SHIFT_VALUE = 0.25
VMEM_LIMIT = 56 * 1024 * 1024
BF16 = jnp.bfloat16
F32 = jnp.float32


def kinetic_taps():
    radius = 14
    values = np.zeros(2 * radius + 1)
    factor = float(math.factorial(radius)) ** 2
    for offset in range(1, radius + 1):
        weight = (
            2.0
            * (-1.0) ** (offset + 1)
            * factor
            / (
                offset
                * offset
                * float(math.factorial(radius - offset))
                * float(math.factorial(radius + offset))
            )
        )
        values[radius + offset] = weight
        values[radius - offset] = weight
    values[radius] = -2.0 * sum((1.0 / float(offset * offset) for offset in range(1, radius + 1)))
    return values


def magic_taps():
    shifted = np.arange(-7, 9) - 0.25
    sinc_values = np.sin(np.pi * shifted) / (np.pi * shifted)
    values = sinc_values * (0.5 + 0.5 * np.cos(np.pi * shifted / 8.5))
    return values / values.sum()


def circulant(values, first, length):
    matrix = np.zeros((length, length))
    for target in range(length):
        for position in range(values.shape[0]):
            matrix[target, (target + first + position) % length] += values[position]
    return matrix


def kinetic_spectrum():
    taps = -KINETIC_SCALE * kinetic_taps()
    offsets = np.arange(-14, 15)
    modes = np.arange(GRID).reshape(GRID, 1)
    return np.cos(2.0 * np.pi * modes * offsets.reshape(1, -1) / GRID) @ taps


def hartley():
    angle = 2.0 * np.pi * np.outer(np.arange(GRID), np.arange(GRID)) / GRID
    return (np.cos(angle) + np.sin(angle)) / np.sqrt(GRID)


def chebyshev_symbol():
    line = kinetic_spectrum()
    low_end = SHIFT_VALUE
    high_end = SHIFT_VALUE + 3.0 * float(line.max())
    centre_value = 0.5 * (high_end + low_end)
    half_width = 0.5 * (high_end - low_end)
    ratio_base = centre_value / half_width
    rho_value = 1.0 / ratio_base
    operator = line[:, None, None] + line[None, :, None] + line[None, None, :] + SHIFT_VALUE
    solution_value = np.zeros_like(operator)
    residual = np.ones_like(operator)
    direction = residual / centre_value
    for counter in range(CHEB):
        solution_value = solution_value + direction
        if counter + 1 < CHEB:
            residual = residual - operator * direction
            rho_next = 1.0 / (2.0 * ratio_base - rho_value)
            direction = rho_next * rho_value * direction + 2.0 * rho_next / half_width * residual
            rho_value = rho_next
    blocks = solution_value.reshape(GRID // 4, 2, 2, PLANES, 2, GRID)
    return blocks.transpose(0, 4, 3, 1, 2, 5).reshape(GRID // 4 * GRID, 256).astype(np.float32)


def split_table(matrix):
    high = np.asarray(matrix, np.float32).astype(jnp.bfloat16)
    low = (np.asarray(matrix, np.float64) - high.astype(np.float64)).astype(np.float32).astype(jnp.bfloat16)
    return high, low


def rows_table(matrix):
    high, low = split_table(matrix)
    return np.concatenate([high, high, low], axis=1)


def columns_table(matrix):
    order = np.concatenate([np.arange(0, GRID, 2), np.arange(1, GRID, 2)])
    return rows_table(matrix[order][:, order])


def lanes_table(matrix):
    high, low = split_table(np.kron(np.eye(2), matrix.T))
    both = np.concatenate([high, low], axis=1)
    return np.concatenate([both, both], axis=0)


def lanes_table_of_two(first, second):
    parts = [split_table(np.kron(np.eye(2), matrix.T)) for matrix in (first, second)]
    high = np.concatenate([part[0] for part in parts], axis=1)
    low = np.concatenate([part[1] for part in parts], axis=1)
    return np.concatenate([high, high, low], axis=0)


def split_pair(value):
    high = value.astype(BF16)
    low = (value - high.astype(F32)).astype(BF16)
    return high, low


def dot32(left, right):
    return jnp.dot(left, right, preferred_element_type=F32)


def along_rows(table, value):
    high, low = split_pair(value)
    return dot32(table, jnp.concatenate([high, low, high], axis=0))


def along_lanes(table, value):
    high, low = split_pair(value)
    product = dot32(jnp.concatenate([high, low], axis=1), table)
    return product[:, :128] + product[:, 128:]


def along_lanes_of_two(table, value):
    high, low = split_pair(value)
    product = dot32(jnp.concatenate([high, low, high], axis=1), table)
    return product[:, :128], product[:, 128:]


def lane_index(shape):
    return lax.broadcasted_iota(jnp.int32, shape, 1)


PITCH = GRID + 1
PITCHED = (PITCH * PLANES, 128)


def x_rows(first):
    return pl.ds(first, PLANES, stride=PITCH)


def turn(first, second):
    half = lane_index((PLANES, 128)) < 64
    return (
        jnp.where(half, first, pltpu.roll(second, 64, 1)),
        jnp.where(half, pltpu.roll(first, 64, 1), second),
    )


def columns_of(ref, first):
    pairs = [
        jnp.concatenate(turn(ref[x_rows(first + shift), :], ref[x_rows(first + shift + 1), :]), axis=0)
        for shift in (0, 2)
    ]
    return jnp.concatenate(pairs, axis=1)


def x_planes(value):
    return (
        *turn(value[:PLANES, :128], value[PLANES:, :128]),
        *turn(value[:PLANES, 128:], value[PLANES:, 128:]),
    )


def put_columns(ref, first, value):
    for shift, plane in enumerate(x_planes(value)):
        ref[x_rows(first + shift), :] = plane


def add_columns(ref, first, value):
    for shift, plane in enumerate(x_planes(value)):
        ref[x_rows(first + shift), :] = ref[x_rows(first + shift), :] + plane


def block_of(plane):
    return pl.ds(pl.multiple_of(plane * GRID, GRID), GRID)


def run_bounds(runs):
    row = lax.broadcasted_iota(jnp.int32, (GRID, PLANES), 0)
    column = lax.broadcasted_iota(jnp.int32, (GRID, PLANES), 1)
    repeat = (row // 2 == column).astype(F32).astype(BF16)
    own = lax.broadcasted_iota(jnp.int32, (GRID, 128), 0) % 2 == lane_index((GRID, 128)) // 64
    bounds = []
    for bound in range(2):
        lines = runs[bound : bound + 1, :].reshape(PLANES, 128).astype(F32).astype(BF16)
        bounds.append(jnp.where(own, dot32(repeat, lines), 0.0))
    return jnp.concatenate(bounds, axis=0).astype(BF16)


def region_pair(bounds, pair):
    lane = lane_index((128, 256))
    line = lax.broadcasted_iota(jnp.int32, (128, 256), 0) % GRID
    pick = (line == lane // 64 + 4 * pair).astype(F32).astype(BF16)
    spread = dot32(bounds, pick)
    depth = (lane_index((GRID, 256)) % GRID).astype(F32)
    return ((depth >= spread[:GRID]) & (depth < spread[GRID:])).astype(F32)


def fold_pair(value):
    first, second = value[:, :128], value[:, 128:]
    lower = (lane_index((GRID, 128)) // 32) % 2 == 0
    return jnp.where(lower, first + pltpu.roll(first, 96, 1), second + pltpu.roll(second, 32, 1))


def unfold_pair(tile):
    lower = (lane_index((GRID, 128)) // 32) % 2 == 0
    first = jnp.where(lower, tile, pltpu.roll(tile, 32, 1))
    second = jnp.where(lower, pltpu.roll(tile, 96, 1), tile)
    return jnp.concatenate([first, second], axis=1)


def load_planes(hbm, vmem, sem):
    for plane in range(PLANES):
        pltpu.make_async_copy(
            hbm.at[:, pl.ds(plane * 128, 128)], vmem.at[pl.ds(plane * GRID, GRID), :], sem
        ).start()


def wait_planes(vmem, sem):
    pltpu.make_async_copy(vmem, vmem, sem).wait()


def pitched_block(plane):
    return pl.ds(plane * PITCH, GRID)


def both_planes(ref, pair, at=pitched_block):
    return jnp.concatenate([ref[at(2 * pair), :], ref[at(2 * pair + 1), :]], axis=1)


def put_both_planes(ref, pair, value, at=pitched_block):
    ref[at(2 * pair), :] = value[:, :128]
    ref[at(2 * pair + 1), :] = value[:, 128:]


def stacked(values):
    return jnp.concatenate([half for value in values for half in (value[:, :128], value[:, 128:])], axis=0)


def unstacked(value):
    return [
        jnp.concatenate([value[row : row + GRID], value[row + GRID : row + 2 * GRID]], axis=1)
        for row in range(0, value.shape[0], 2 * GRID)
    ]


GROUP = 4
GROUPS = PLANES // 2 // GROUP


def pairs_of(group):
    return [group * GROUP + member for member in range(GROUP)]


def hamiltonian_head(kinetic, forward, tables, group, values):
    lanes_kf, rows_k, rows_f = tables
    along, magic = along_lanes_of_two(lanes_kf[...], stacked(values))
    for pair, value, first, second in zip(pairs_of(group), values, unstacked(along), unstacked(magic)):
        put_both_planes(kinetic, pair, first + along_rows(rows_k[...], value))
        put_both_planes(forward, pair, along_rows(rows_f[...], second))


def hamiltonian_middle(masked, kinetic, forward, potential, tables, step):
    columns_k, columns_f, columns_b = tables
    first = 4 * step
    real = along_rows(columns_f[...], columns_of(forward, first))
    weighted = real * columns_of(potential, first)
    put_columns(forward, first, along_rows(columns_b[...], weighted))
    add_columns(kinetic, first, along_rows(columns_k[...], columns_of(masked, first)))


def hamiltonian_tail(kinetic, forward, tables, group):
    rows_b, lanes_b = tables
    values = [along_rows(rows_b[...], both_planes(forward, pair)) for pair in pairs_of(group)]
    returned = unstacked(along_lanes(lanes_b[...], stacked(values)))
    return [both_planes(kinetic, pair) + value for pair, value in zip(pairs_of(group), returned)]


def loop(count, body, unroll=1):
    def step(index, carry):
        body(index)
        return carry

    lax.fori_loop(0, count, step, 0, unroll=unroll)


def precondition_kernel(
    tiles_hbm, region_hbm, lanes_q, rows_q, columns_q, symbol_hbm, gradient_out, preconditioned_out,
    tiles, region, gradient, work, symbol, load_sems, sems,
):
    def fetch(group):
        rows = pl.ds(group * GROUP * GRID, GROUP * GRID)
        planes = pl.ds(group * GROUP * 2 * GRID, GROUP * 2 * GRID)
        return (
            pltpu.make_async_copy(tiles_hbm.at[rows], tiles.at[rows], load_sems.at[0, group]),
            pltpu.make_async_copy(region_hbm.at[planes], region.at[planes], load_sems.at[1, group]),
        )

    for group in range(GROUPS):
        for copy in fetch(group):
            copy.start()
    symbol_copy = pltpu.make_async_copy(symbol_hbm, symbol, sems.at[0])
    symbol_copy.start()

    def put(buffer, target, pair, sem):
        for plane in (2 * pair, 2 * pair + 1):
            pltpu.make_async_copy(
                buffer.at[block_of(plane), :],
                target.at[0, :, pl.ds(pl.multiple_of(plane * 128, 128), 128)],
                sem,
            ).start()

    def head(group):
        for copy in fetch(group):
            copy.wait()
        values = []
        for pair in pairs_of(group):
            value = unfold_pair(tiles[block_of(pair), :]) * both_planes(region, pair, block_of)
            put_both_planes(gradient, pair, value, block_of)
            put(gradient, gradient_out, pair, sems.at[1])
            values.append(value)
        turned = unstacked(along_lanes(lanes_q[...], stacked(values)))
        for pair, value in zip(pairs_of(group), turned):
            put_both_planes(work, pair, along_rows(rows_q[...], value))

    loop(GROUPS, head)
    symbol_copy.wait()

    def middle(step):
        first = 4 * step
        modes = along_rows(columns_q[...], columns_of(work, first)) * symbol[block_of(step), :]
        put_columns(work, first, along_rows(columns_q[...], modes))

    loop(GRID // 4, middle, MIDDLE_UNROLL)
    wait_planes(gradient, sems.at[1])

    def tail(group):
        values = [along_rows(rows_q[...], both_planes(work, pair)) for pair in pairs_of(group)]
        turned = unstacked(along_lanes(lanes_q[...], stacked(values)))
        for pair, value in zip(pairs_of(group), turned):
            put_both_planes(gradient, pair, value * both_planes(region, pair, block_of), block_of)
            put(gradient, preconditioned_out, pair, sems.at[2])

    loop(GROUPS, tail)
    wait_planes(gradient, sems.at[2])


MIDDLE_UNROLL = 2


def in_vmem(count):
    return [pl.BlockSpec(memory_space=pltpu.VMEM)] * count


def anywhere(count):
    return [pl.BlockSpec(memory_space=pl.ANY)] * count


FIELD = (GRID * PLANES, 128)
TILES = (8 * DEVICES, 128)


def precondition(tiles, region):
    modes = hartley()
    field = pltpu.VMEM(FIELD, F32)
    pitched = pltpu.VMEM(PITCHED, F32)
    shape = jax.ShapeDtypeStruct((1, GRID, GRID * GRID), F32)
    return pl.pallas_call(
        precondition_kernel,
        out_shape=(shape, shape),
        in_specs=anywhere(2) + in_vmem(3) + anywhere(1),
        out_specs=anywhere(2),
        scratch_shapes=[
            pltpu.VMEM(TILES, F32), field, field, pitched, pltpu.VMEM((GRID // 4 * GRID, 256), F32),
            pltpu.SemaphoreType.DMA((2, GROUPS)),
            pltpu.SemaphoreType.DMA((3,)),
        ],
        compiler_params=pltpu.CompilerParams(vmem_limit_bytes=VMEM_LIMIT),
        name="precondition",
    )(
        tiles,
        region,
        jnp.asarray(lanes_table(modes)),
        jnp.asarray(rows_table(modes)),
        jnp.asarray(columns_table(modes)),
        jnp.asarray(chebyshev_symbol()),
    )


def hamiltonian_tables():
    kinetic = -KINETIC_SCALE * circulant(kinetic_taps(), -14, GRID)
    magic = circulant(magic_taps(), -7, GRID)
    tables = (
        lanes_table_of_two(kinetic, magic),
        rows_table(kinetic),
        rows_table(magic),
        columns_table(kinetic),
        columns_table(magic),
        columns_table(magic.T),
        rows_table(magic.T),
        lanes_table(magic.T),
    )
    return [jnp.asarray(table) for table in tables]


def tile_of(index):
    return pl.ds(pl.multiple_of(index * 8, 8), 8)


def row_of(index):
    return pl.ds(index, 1)


def gradient_kernel(
    wave, potential_hbm, runs, lanes_kf, rows_k, rows_f, columns_k, columns_f, columns_b, rows_b, lanes_b,
    gradient_tiles, region_out,
    waves, staged, region, masked, kinetic, forward, potential,
    masked_send, masked_recv, applied_send, applied_recv, back_send,
    partial, gathered, row, matrix,
    load_sems, send_sems, recv_sems,
):
    me = lax.axis_index("orb") * 2 + lax.axis_index("pair")
    barrier = pltpu.get_barrier_semaphore()

    def peer_at(step):
        return jnp.bitwise_and(me + step, DEVICES - 1)

    def greet(step):
        pl.semaphore_signal(barrier, inc=1, device_id=peer_at(step + 1), device_id_type=LOGICAL)

    load_planes(wave.at[0], waves, load_sems.at[0])
    loop(DEVICES - 1, greet, SEND_UNROLL)
    load_planes(potential_hbm, staged, load_sems.at[1])
    bounds = run_bounds(runs[...])
    wait_planes(waves, load_sems.at[0])

    def send(source, target, phase, peer, source_at, target_at):
        pltpu.make_async_remote_copy(
            src_ref=source.at[source_at(peer)],
            dst_ref=target.at[target_at(me)],
            send_sem=send_sems.at[phase],
            recv_sem=recv_sems.at[phase],
            device_id=peer,
            device_id_type=LOGICAL,
        ).start()

    def scatter(source, target, phase, source_at, target_at):
        loop(
            DEVICES - 1,
            lambda step: send(source, target, phase, peer_at(step + 1), source_at, target_at),
            SEND_UNROLL,
        )

    def drain(buffer, sem):
        whole = buffer.at[pl.ds(0, buffer.shape[0] * (DEVICES - 1) // DEVICES)]
        pltpu.make_async_copy(whole, whole, sem).wait()

    def head(group):
        values = []
        for pair in pairs_of(group):
            mask = region_pair(bounds, pair)
            put_both_planes(region, pair, mask, block_of)
            value = both_planes(waves, pair, block_of) * mask
            put_both_planes(masked, pair, value)
            masked_send[block_of(pair), :] = fold_pair(value)
            values.append(value)
        hamiltonian_head(kinetic, forward, (lanes_kf, rows_k, rows_f), group, values)

    loop(GROUPS, head)
    region_copy = pltpu.make_async_copy(region, region_out, load_sems.at[2])
    region_copy.start()
    wait_planes(staged, load_sems.at[1])

    def pitch(pair):
        put_both_planes(potential, pair, both_planes(staged, pair, block_of))

    loop(PLANES // 2, pitch, 4)
    pl.semaphore_wait(barrier, DEVICES - 1)

    def middle(step):
        hamiltonian_middle(
            masked, kinetic, forward, potential, (columns_k, columns_f, columns_b), step
        )

    def middle_sending(step):
        for sub in range(9):
            send(masked_send, masked_recv, 0, peer_at(9 * step + sub + 1), tile_of, tile_of)
        middle(step)

    loop(14, middle_sending, MIDDLE_UNROLL)
    send(masked_send, masked_recv, 0, peer_at(127), tile_of, tile_of)
    middle(14)
    middle(15)
    masked_recv[tile_of(me), :] = masked_send[tile_of(me), :]

    def tail(step, sends):
        group = jnp.bitwise_and(lax.shift_right_logical(me, GROUP_SHIFT) + (step + 1), GROUPS - 1)
        values = hamiltonian_tail(kinetic, forward, (rows_b, lanes_b), group)
        for pair, value in zip(pairs_of(group), values):
            applied_send[block_of(pair), :] = fold_pair(value * both_planes(region, pair, block_of))
        for sub in range(sends):
            peer = 8 * GROUP * group + jnp.bitwise_and(me + (sub + 1), 8 * GROUP - 1)
            send(applied_send, applied_recv, 1, peer, tile_of, tile_of)

    loop(GROUPS - 1, lambda step: tail(step, 8 * GROUP))
    tail(GROUPS - 1, 8 * GROUP - 1)
    applied_recv[tile_of(me), :] = applied_send[tile_of(me), :]
    drain(masked_recv, recv_sems.at[0])
    drain(applied_recv, recv_sems.at[1])

    total = jnp.zeros((2 * DEVICES, 2 * DEVICES), F32)
    for sub in range(0, 8, 2):
        left = []
        right = []
        for one in (sub, sub + 1):
            rows = pl.ds(one, DEVICES, stride=8)
            left.append(jnp.concatenate(split_pair(applied_recv[rows, :]), axis=0))
            right.append(jnp.concatenate(split_pair(masked_recv[rows, :]), axis=0))
        total = total + lax.dot_general(
            jnp.concatenate(left, axis=1),
            jnp.concatenate(right, axis=1),
            (((1,), (1,)), ((), ())),
            preferred_element_type=F32,
        )
    partial[:, 0, :] = (
        total[:DEVICES, :DEVICES] + (total[:DEVICES, DEVICES:] + total[DEVICES:, :DEVICES])
    )
    scatter(partial, gathered, 2, row_of, row_of)
    gathered[row_of(me)] = partial[row_of(me)]
    drain(gathered, recv_sems.at[2])
    row[...] = jnp.sum(gathered[...], axis=0, keepdims=True) * (1.0 / CELLS)
    scatter(row, matrix, 3, lambda peer: pl.ds(0, 1), row_of)
    matrix[row_of(me)] = row[...]
    drain(matrix, recv_sems.at[3])
    matrix_high, matrix_low = split_pair(matrix[:, 0, :])
    table = jnp.concatenate([matrix_high, matrix_high, matrix_low], axis=1)
    for sub in range(0, 8, 2):
        here = pl.ds(sub, DEVICES, stride=8)
        there = pl.ds(sub + 1, DEVICES, stride=8)
        projected = along_rows(
            table, jnp.concatenate([masked_recv[here, :], masked_recv[there, :]], axis=1)
        )
        back_send[here, :] = applied_recv[here, :] - projected[:, :128]
        back_send[there, :] = applied_recv[there, :] - projected[:, 128:]
    scatter(back_send, gradient_tiles, 4, tile_of, tile_of)
    gradient_tiles[tile_of(me), :] = back_send[tile_of(me), :]
    region_copy.wait()
    drain(masked_send, send_sems.at[0])
    drain(applied_send, send_sems.at[1])
    drain(partial, send_sems.at[2])
    drain(matrix, send_sems.at[3])
    drain(gradient_tiles, recv_sems.at[4])
    drain(back_send, send_sems.at[4])


SEND_UNROLL = 8
GROUP_SHIFT = 5
LOGICAL = pl.DeviceIdType.LOGICAL


def gradient_fields(wavefunctions, potential, line_runs):
    field = pltpu.VMEM(FIELD, F32)
    pitched = pltpu.VMEM(PITCHED, F32)
    tiles = pltpu.VMEM(TILES, F32)
    rows = pltpu.VMEM((DEVICES, 1, 128), F32)
    return pl.pallas_call(
        gradient_kernel,
        out_shape=(jax.ShapeDtypeStruct(TILES, F32), jax.ShapeDtypeStruct(FIELD, F32)),
        in_specs=anywhere(2) + in_vmem(9),
        out_specs=in_vmem(1) + anywhere(1),
        scratch_shapes=[
            field, field, field, pitched, pitched, pitched, pitched,
            tiles, tiles, tiles, tiles, tiles,
            rows, rows, pltpu.VMEM((1, 1, 128), F32), rows,
            pltpu.SemaphoreType.DMA((3,)),
            pltpu.SemaphoreType.DMA((5,)),
            pltpu.SemaphoreType.DMA((5,)),
        ],
        compiler_params=pltpu.CompilerParams(
            collective_id=0, has_side_effects=True, vmem_limit_bytes=VMEM_LIMIT
        ),
        name="gradient",
    )(wavefunctions, potential, line_runs, *hamiltonian_tables())


def on_device(wavefunctions, potential, line_runs):
    tiles, region = gradient_fields(wavefunctions, potential, line_runs)
    return precondition(tiles, region)


def solution(mesh):
    return jax.shard_map(
        on_device,
        mesh=mesh,
        in_specs=(P(("orb", "pair"), None, None), P(), P()),
        out_specs=(P(("orb", "pair"), None, None), P(("orb", "pair"), None, None)),
        check_vma=False,
    )
```

time: 84.6 us -> 65.2 us (0.77)
  Pallas kernels: 83 us -> 63.6 us
    pallas_call x2, Pallas kernels: 83 us -> 63.6 us  [the longest x1 53.6 us: gradient_fields(): pl.pallas_call(gradient_kernel, out_shape=(jax.ShapeDtypeStruct(TILES, F3...]
where the time goes in v2:
time: 65.2 us; the launch traced here: 64.3 us
  Pallas kernels  63.6 us (98%)
    pallas_call x1, Pallas kernels, gradient_fields(): pl.pallas_call(gradient_kernel, out_shape=(jax.ShapeDtypeStruct(TILES, F3...  53.6 us
    pallas_call x1, Pallas kernels, precondition(): pl.pallas_call(precondition_kernel, out_shape=(shape, shape), in_specs=an...  10 us

profile of v2, /device:TPU:0, one launch (start us, length us, event | category | flops | bytes accessed | tf_op | source)
XLA Modules:
  0.0 64.3 jit_solution(17748403710948383695)
XLA Ops:
  0.6 53.6 %gradient.1 = (f32[1024,128]{1,0:T(8,128)}, f32[2048,128]{1,0:T(8,128)}) custom-call(f32[1,64,4096]{2,1,0:T(8,128)} %wave.1, f32[64,4096]{1,0:T(8,128)} %potential_hbm.1, s32[2,4096]{1,0:T(2,128)} %runs.1, bf16[384,256]{1,0:T(8,128)(2,1)} %constant.24.clone.lanes_kf, bf16[64,192]{1,0:T(8,128)(2,1)} %constant.25.clone.rows_k, ...), custom_call_target="tpu_custom_call" | custom-call | tf_op jit(solution)/shard_map/gradient/pallas_call | solution.py:589
  54.2 10.0 %precondition.1 = (f32[1,64,4096]{2,1,0:T(8,128)}, f32[1,64,4096]{2,1,0:T(8,128)}) custom-call(f32[1024,128]{1,0:T(8,128)} %get-tuple-element.4.tiles_hbm, f32[2048,128]{1,0:T(8,128)} %get-tuple-element.5.region_hbm, bf16[256,256]{1,0:T(8,128)(2,1)} %constant.32.clone.lanes_q, bf16[64,192]{1,0:T(8,128)(2,1)} %constant.33.clone.rows_q, ...), custom_call_target="tpu_custom_call" | custom-call | tf_op jit(solution)/shard_map/precondition/pallas_call | solution.py:391

commit v3 on v2

--- a/solution.py
+++ b/solution.py
@@ -13,7 +13,6 @@
 CELLS = GRID * GRID * GRID
 PLANES = GRID // 2
 DEVICES = 128
-MESH_IDS = pl.DeviceIdType.MESH
 KINETIC_SCALE = 0.125
 SHIFT_VALUE = 0.25
 VMEM_LIMIT = 56 * 1024 * 1024
@@ -434,22 +433,29 @@
     return pl.ds(index, 1)
 
 
+TEAMS = 4
+TEAM = DEVICES // TEAMS
+LOGICAL = pl.DeviceIdType.LOGICAL
+SEND_UNROLL = 8
+
+
 def gradient_kernel(
     wave, potential_hbm, runs, lanes_kf, rows_k, rows_f, columns_k, columns_f, columns_b, rows_b, lanes_b,
     gradient_tiles, region_out,
     waves, staged, region, masked, kinetic, forward, potential,
     masked_send, masked_recv, applied_send, applied_recv, back_send,
-    partial, gathered, row, matrix,
+    masked_split, partial, gathered, row, matrix,
     load_sems, send_sems, recv_sems,
 ):
-    me = lax.axis_index("orb") * 2 + lax.axis_index("pair")
+    device = lax.axis_index("orb") * 2 + lax.axis_index("pair")
+    my_team = jnp.bitwise_and(device, TEAMS - 1)
+    my_seat = lax.shift_right_logical(device, 2)
+    me = my_team * TEAM + my_seat
     barrier = pltpu.get_barrier_semaphore()
 
-    def peer_at(step):
-        return jnp.bitwise_and(me + step, DEVICES - 1)
-
     def greet(step):
-        pl.semaphore_signal(barrier, inc=1, device_id=peer_at(step + 1), device_id_type=LOGICAL)
+        peer = jnp.bitwise_and(device + (step + 1), DEVICES - 1)
+        pl.semaphore_signal(barrier, inc=1, device_id=peer, device_id_type=LOGICAL)
 
     load_planes(wave.at[0], waves, load_sems.at[0])
     loop(DEVICES - 1, greet, SEND_UNROLL)
@@ -457,25 +463,37 @@
     bounds = run_bounds(runs[...])
     wait_planes(waves, load_sems.at[0])
 
-    def send(source, target, phase, peer, source_at, target_at):
-        pltpu.make_async_remote_copy(
-            src_ref=source.at[source_at(peer)],
-            dst_ref=target.at[target_at(me)],
-            send_sem=send_sems.at[phase],
-            recv_sem=recv_sems.at[phase],
-            device_id=peer,
-            device_id_type=LOGICAL,
-        ).start()
-
-    def scatter(source, target, phase, source_at, target_at):
-        loop(
-            DEVICES - 1,
-            lambda step: send(source, target, phase, peer_at(step + 1), source_at, target_at),
-            SEND_UNROLL,
-        )
-
-    def drain(buffer, sem):
-        whole = buffer.at[pl.ds(0, buffer.shape[0] * (DEVICES - 1) // DEVICES)]
+    def team_after(stage):
+        return jnp.bitwise_and(my_team + (stage + 1), TEAMS - 1)
+
+    def team_before(stage):
+        return jnp.bitwise_and(my_team + (TEAMS - 1 - stage), TEAMS - 1)
+
+    def send_team(source, target, phase, team, count, source_at, target_at, signal):
+        def send(step):
+            seat = jnp.bitwise_and(my_seat + (step + 1), TEAM - 1)
+            pltpu.make_async_remote_copy(
+                src_ref=source.at[source_at(team * TEAM + seat)],
+                dst_ref=target.at[target_at(me)],
+                send_sem=send_sems.at[phase],
+                recv_sem=recv_sems.at[phase, signal],
+                device_id=seat * TEAMS + team,
+                device_id_type=LOGICAL,
+            ).start()
+
+        loop(count, send, SEND_UNROLL)
+
+    def size_of(stage):
+        return TEAM if stage < TEAMS - 1 else TEAM - 1
+
+    def scatter(source, target, phase, source_at, target_at, signal=0):
+        for stage in range(TEAMS):
+            send_team(
+                source, target, phase, team_after(stage), size_of(stage), source_at, target_at, signal
+            )
+
+    def drain(buffer, sem, count=DEVICES - 1):
+        whole = buffer.at[pl.ds(0, buffer.shape[0] * count // DEVICES)]
         pltpu.make_async_copy(whole, whole, sem).wait()
 
     def head(group):
@@ -499,86 +517,85 @@
 
     loop(PLANES // 2, pitch, 4)
     pl.semaphore_wait(barrier, DEVICES - 1)
+    scatter(masked_send, masked_recv, 0, tile_of, tile_of)
+    masked_recv[tile_of(me), :] = masked_send[tile_of(me), :]
 
     def middle(step):
         hamiltonian_middle(
             masked, kinetic, forward, potential, (columns_k, columns_f, columns_b), step
         )
 
-    def middle_sending(step):
-        for sub in range(9):
-            send(masked_send, masked_recv, 0, peer_at(9 * step + sub + 1), tile_of, tile_of)
-        middle(step)
-
-    loop(14, middle_sending, MIDDLE_UNROLL)
-    send(masked_send, masked_recv, 0, peer_at(127), tile_of, tile_of)
-    middle(14)
-    middle(15)
-    masked_recv[tile_of(me), :] = masked_send[tile_of(me), :]
-
-    def tail(step, sends):
-        group = jnp.bitwise_and(lax.shift_right_logical(me, GROUP_SHIFT) + (step + 1), GROUPS - 1)
-        values = hamiltonian_tail(kinetic, forward, (rows_b, lanes_b), group)
-        for pair, value in zip(pairs_of(group), values):
+    loop(GRID // 4, middle, MIDDLE_UNROLL)
+
+    def tail(stage, count):
+        team = team_after(stage)
+        values = hamiltonian_tail(kinetic, forward, (rows_b, lanes_b), team)
+        for pair, value in zip(pairs_of(team), values):
             applied_send[block_of(pair), :] = fold_pair(value * both_planes(region, pair, block_of))
-        for sub in range(sends):
-            peer = 8 * GROUP * group + jnp.bitwise_and(me + (sub + 1), 8 * GROUP - 1)
-            send(applied_send, applied_recv, 1, peer, tile_of, tile_of)
-
-    loop(GROUPS - 1, lambda step: tail(step, 8 * GROUP))
-    tail(GROUPS - 1, 8 * GROUP - 1)
+        send_team(applied_send, applied_recv, 1, team, count, tile_of, tile_of, my_team)
+
+    loop(TEAMS - 1, lambda stage: tail(stage, TEAM))
+    tail(TEAMS - 1, TEAM - 1)
     applied_recv[tile_of(me), :] = applied_send[tile_of(me), :]
-    drain(masked_recv, recv_sems.at[0])
-    drain(applied_recv, recv_sems.at[1])
-
-    total = jnp.zeros((2 * DEVICES, 2 * DEVICES), F32)
-    for sub in range(0, 8, 2):
-        left = []
-        right = []
-        for one in (sub, sub + 1):
-            rows = pl.ds(one, DEVICES, stride=8)
-            left.append(jnp.concatenate(split_pair(applied_recv[rows, :]), axis=0))
-            right.append(jnp.concatenate(split_pair(masked_recv[rows, :]), axis=0))
-        total = total + lax.dot_general(
-            jnp.concatenate(left, axis=1),
-            jnp.concatenate(right, axis=1),
-            (((1,), (1,)), ((), ())),
-            preferred_element_type=F32,
+    drain(masked_recv, recv_sems.at[0, 0])
+    for sub in range(8):
+        high, low = split_pair(masked_recv[pl.ds(sub, DEVICES, stride=8), :])
+        masked_split[:DEVICES, sub * 128 : sub * 128 + 128] = high
+        masked_split[DEVICES:, sub * 128 : sub * 128 + 128] = low
+
+    def strided(team, sub):
+        return pl.ds(team * (TEAM * 8) + sub, TEAM, stride=8)
+
+    def correlate(stage, count):
+        team = team_before(stage)
+        drain(applied_recv, recv_sems.at[1, team], count)
+        parts = [split_pair(applied_recv[strided(team, sub), :]) for sub in range(8)]
+        left = jnp.concatenate(
+            [jnp.concatenate([part[which] for part in parts], axis=1) for which in range(2)], axis=0
         )
-    partial[:, 0, :] = (
-        total[:DEVICES, :DEVICES] + (total[:DEVICES, DEVICES:] + total[DEVICES:, :DEVICES])
-    )
-    scatter(partial, gathered, 2, row_of, row_of)
+        total = lax.dot_general(
+            left, masked_split[...], (((1,), (1,)), ((), ())), preferred_element_type=F32
+        )
+        rows = total[:TEAM, :DEVICES] + (total[:TEAM, DEVICES:] + total[TEAM:, :DEVICES])
+        partial[pl.ds(team * TEAM, TEAM), 0, :] = rows
+        send_team(partial, gathered, 2, team, count, row_of, row_of, 0)
+
+    loop(TEAMS - 1, lambda stage: correlate(stage, TEAM))
+    correlate(TEAMS - 1, TEAM - 1)
     gathered[row_of(me)] = partial[row_of(me)]
-    drain(gathered, recv_sems.at[2])
+    drain(gathered, recv_sems.at[2, 0])
     row[...] = jnp.sum(gathered[...], axis=0, keepdims=True) * (1.0 / CELLS)
-    scatter(row, matrix, 3, lambda peer: pl.ds(0, 1), row_of)
+    scatter(row, matrix, 3, lambda peer: pl.ds(0, 1), row_of, my_team)
     matrix[row_of(me)] = row[...]
-    drain(matrix, recv_sems.at[3])
-    matrix_high, matrix_low = split_pair(matrix[:, 0, :])
-    table = jnp.concatenate([matrix_high, matrix_high, matrix_low], axis=1)
-    for sub in range(0, 8, 2):
-        here = pl.ds(sub, DEVICES, stride=8)
-        there = pl.ds(sub + 1, DEVICES, stride=8)
-        projected = along_rows(
-            table, jnp.concatenate([masked_recv[here, :], masked_recv[there, :]], axis=1)
-        )
-        back_send[here, :] = applied_recv[here, :] - projected[:, :128]
-        back_send[there, :] = applied_recv[there, :] - projected[:, 128:]
-    scatter(back_send, gradient_tiles, 4, tile_of, tile_of)
+
+    def project(stage, count):
+        team = team_before(stage)
+        drain(matrix, recv_sems.at[3, team], count)
+        high, low = split_pair(matrix[pl.ds(team * TEAM, TEAM), 0, :])
+        table = jnp.concatenate([high, high, low], axis=1)
+        for sub in range(0, 8, 2):
+            lanes = slice(sub * 128, sub * 128 + 256)
+            projected = dot32(
+                table,
+                jnp.concatenate([masked_split[:, lanes], masked_split[:DEVICES, lanes]], axis=0),
+            )
+            for shift in range(2):
+                rows = strided(team, sub + shift)
+                back_send[rows, :] = (
+                    applied_recv[rows, :] - projected[:, shift * 128 : shift * 128 + 128]
+                )
+        send_team(back_send, gradient_tiles, 4, team, count, tile_of, tile_of, 0)
+
+    loop(TEAMS - 1, lambda stage: project(stage, TEAM))
+    project(TEAMS - 1, TEAM - 1)
     gradient_tiles[tile_of(me), :] = back_send[tile_of(me), :]
     region_copy.wait()
     drain(masked_send, send_sems.at[0])
     drain(applied_send, send_sems.at[1])
     drain(partial, send_sems.at[2])
     drain(matrix, send_sems.at[3])
-    drain(gradient_tiles, recv_sems.at[4])
+    drain(gradient_tiles, recv_sems.at[4, 0])
     drain(back_send, send_sems.at[4])
-
-
-SEND_UNROLL = 8
-GROUP_SHIFT = 5
-LOGICAL = pl.DeviceIdType.LOGICAL
 
 
 def gradient_fields(wavefunctions, potential, line_runs):
@@ -594,10 +611,11 @@
         scratch_shapes=[
             field, field, field, pitched, pitched, pitched, pitched,
             tiles, tiles, tiles, tiles, tiles,
+            pltpu.VMEM((2 * DEVICES, 8 * 128), BF16),
             rows, rows, pltpu.VMEM((1, 1, 128), F32), rows,
             pltpu.SemaphoreType.DMA((3,)),
             pltpu.SemaphoreType.DMA((5,)),
-            pltpu.SemaphoreType.DMA((5,)),
+            pltpu.SemaphoreType.DMA((5, TEAMS)),
         ],
         compiler_params=pltpu.CompilerParams(
             collective_id=0, has_side_effects=True, vmem_limit_bytes=VMEM_LIMIT

time: 65.2 us -> 61.9 us (0.949)
  Pallas kernels: 63.6 us -> 60 us
    pallas_call x1, Pallas kernels: 53.6 us -> 50 us  [gradient_fields(): pl.pallas_call(gradient_kernel, out_shape=(jax.ShapeDtypeStruct(TILES, F3...]
where the time goes in v3:
time: 61.9 us; the launch traced here: 60.6 us
  Pallas kernels  60 us (97%)
  between operations  0.64 us (1%)
    pallas_call x1, Pallas kernels, gradient_fields(): pl.pallas_call(gradient_kernel, out_shape=(jax.ShapeDtypeStruct(TILES, F3...  50 us
    pallas_call x1, Pallas kernels, precondition(): pl.pallas_call(precondition_kernel, out_shape=(shape, shape), in_specs=an...  10 us

profile of v3, /device:TPU:0, one launch (start us, length us, event | category | flops | bytes accessed | tf_op | source)
XLA Modules:
  0.0 60.6 jit_solution(4093687874327104693)
XLA Ops:
  0.6 50.0 %gradient.1 = (f32[1024,128]{1,0:T(8,128)}, f32[2048,128]{1,0:T(8,128)}) custom-call(f32[1,64,4096]{2,1,0:T(8,128)} %wave.1, f32[64,4096]{1,0:T(8,128)} %potential_hbm.1, s32[2,4096]{1,0:T(2,128)} %runs.1, bf16[384,256]{1,0:T(8,128)(2,1)} %constant.24.clone.lanes_kf, bf16[64,192]{1,0:T(8,128)(2,1)} %constant.25.clone.rows_k, ...), custom_call_target="tpu_custom_call" | custom-call | tf_op jit(solution)/shard_map/gradient/pallas_call | solution.py:606
  50.6 10.0 %precondition.1 = (f32[1,64,4096]{2,1,0:T(8,128)}, f32[1,64,4096]{2,1,0:T(8,128)}) custom-call(f32[1024,128]{1,0:T(8,128)} %get-tuple-element.4.tiles_hbm, f32[2048,128]{1,0:T(8,128)} %get-tuple-element.5.region_hbm, bf16[256,256]{1,0:T(8,128)(2,1)} %constant.32.clone.lanes_q, bf16[64,192]{1,0:T(8,128)(2,1)} %constant.33.clone.rows_q, ...), custom_call_target="tpu_custom_call" | custom-call | tf_op jit(solution)/shard_map/precondition/pallas_call | solution.py:390

commit v4 on v3

--- a/solution.py
+++ b/solution.py
@@ -345,7 +345,7 @@
         for pair, value in zip(pairs_of(group), turned):
             put_both_planes(work, pair, along_rows(rows_q[...], value))
 
-    loop(GROUPS, head)
+    loop(GROUPS, head, GROUPS)
     symbol_copy.wait()
 
     def middle(step):
@@ -363,11 +363,11 @@
             put_both_planes(gradient, pair, value * both_planes(region, pair, block_of), block_of)
             put(gradient, preconditioned_out, pair, sems.at[2])
 
-    loop(GROUPS, tail)
+    loop(GROUPS, tail, GROUPS)
     wait_planes(gradient, sems.at[2])
 
 
-MIDDLE_UNROLL = 2
+MIDDLE_UNROLL = GRID // 4
 
 
 def in_vmem(count):
@@ -426,7 +426,7 @@
 
 
 def tile_of(index):
-    return pl.ds(pl.multiple_of(index * 8, 8), 8)
+    return pl.ds(pl.multiple_of(index * BLOCK, BLOCK), BLOCK)
 
 
 def row_of(index):
@@ -434,7 +434,9 @@
 
 
 TEAMS = 4
-TEAM = DEVICES // TEAMS
+CHIPS = DEVICES // 2
+TEAM = CHIPS // TEAMS
+BLOCK = 16
 LOGICAL = pl.DeviceIdType.LOGICAL
 SEND_UNROLL = 8
 
@@ -447,18 +449,24 @@
     masked_split, partial, gathered, row, matrix,
     load_sems, send_sems, recv_sems,
 ):
-    device = lax.axis_index("orb") * 2 + lax.axis_index("pair")
-    my_team = jnp.bitwise_and(device, TEAMS - 1)
-    my_seat = lax.shift_right_logical(device, 2)
+    chip = lax.axis_index("orb")
+    core = lax.axis_index("pair")
+    my_team = jnp.bitwise_and(lax.shift_right_logical(chip, 1), 2) + jnp.bitwise_and(chip, 1)
+    my_seat = jnp.bitwise_and(lax.shift_right_logical(chip, 2), 14) + jnp.bitwise_and(
+        lax.shift_right_logical(chip, 1), 1
+    )
     me = my_team * TEAM + my_seat
+    my_half = core * CHIPS
     barrier = pltpu.get_barrier_semaphore()
 
     def greet(step):
-        peer = jnp.bitwise_and(device + (step + 1), DEVICES - 1)
+        peer = jnp.bitwise_and(chip + (step + 1), CHIPS - 1) * 2 + core
         pl.semaphore_signal(barrier, inc=1, device_id=peer, device_id_type=LOGICAL)
 
     load_planes(wave.at[0], waves, load_sems.at[0])
-    loop(DEVICES - 1, greet, SEND_UNROLL)
+    loop(CHIPS - 1, greet, SEND_UNROLL)
+    partner = chip * 2 + (1 - core)
+    pl.semaphore_signal(barrier, inc=1, device_id=partner, device_id_type=LOGICAL)
     load_planes(potential_hbm, staged, load_sems.at[1])
     bounds = run_bounds(runs[...])
     wait_planes(waves, load_sems.at[0])
@@ -470,6 +478,8 @@
         return jnp.bitwise_and(my_team + (TEAMS - 1 - stage), TEAMS - 1)
 
     def send_team(source, target, phase, team, count, source_at, target_at, signal):
+        base = jnp.bitwise_and(team, 2) * 4 + jnp.bitwise_and(team, 1) * 2 + core
+
         def send(step):
             seat = jnp.bitwise_and(my_seat + (step + 1), TEAM - 1)
             pltpu.make_async_remote_copy(
@@ -477,7 +487,7 @@
                 dst_ref=target.at[target_at(me)],
                 send_sem=send_sems.at[phase],
                 recv_sem=recv_sems.at[phase, signal],
-                device_id=seat * TEAMS + team,
+                device_id=jnp.bitwise_and(seat, 14) * 8 + jnp.bitwise_and(seat, 1) * 4 + base,
                 device_id_type=LOGICAL,
             ).start()
 
@@ -492,8 +502,8 @@
                 source, target, phase, team_after(stage), size_of(stage), source_at, target_at, signal
             )
 
-    def drain(buffer, sem, count=DEVICES - 1):
-        whole = buffer.at[pl.ds(0, buffer.shape[0] * count // DEVICES)]
+    def drain(buffer, sem, count=CHIPS - 1):
+        whole = buffer.at[pl.ds(0, buffer.shape[0] * count // CHIPS)]
         pltpu.make_async_copy(whole, whole, sem).wait()
 
     def head(group):
@@ -507,7 +517,7 @@
             values.append(value)
         hamiltonian_head(kinetic, forward, (lanes_kf, rows_k, rows_f), group, values)
 
-    loop(GROUPS, head)
+    loop(GROUPS, head, GROUPS)
     region_copy = pltpu.make_async_copy(region, region_out, load_sems.at[2])
     region_copy.start()
     wait_planes(staged, load_sems.at[1])
@@ -516,9 +526,9 @@
         put_both_planes(potential, pair, both_planes(staged, pair, block_of))
 
     loop(PLANES // 2, pitch, 4)
-    pl.semaphore_wait(barrier, DEVICES - 1)
-    scatter(masked_send, masked_recv, 0, tile_of, tile_of)
-    masked_recv[tile_of(me), :] = masked_send[tile_of(me), :]
+    pl.semaphore_wait(barrier, CHIPS)
+    scatter(masked_send, masked_recv, 0, tile_of, lambda label: tile_of(my_half + label))
+    masked_recv[tile_of(my_half + me), :] = masked_send[tile_of(me), :]
 
     def middle(step):
         hamiltonian_middle(
@@ -537,19 +547,33 @@
     loop(TEAMS - 1, lambda stage: tail(stage, TEAM))
     tail(TEAMS - 1, TEAM - 1)
     applied_recv[tile_of(me), :] = applied_send[tile_of(me), :]
-    drain(masked_recv, recv_sems.at[0, 0])
-    for sub in range(8):
-        high, low = split_pair(masked_recv[pl.ds(sub, DEVICES, stride=8), :])
-        masked_split[:DEVICES, sub * 128 : sub * 128 + 128] = high
-        masked_split[DEVICES:, sub * 128 : sub * 128 + 128] = low
+    drain(masked_recv.at[pl.ds(0, CHIPS * BLOCK)], recv_sems.at[0, 0])
+    kind = masked_recv.at[pl.ds(pl.multiple_of(my_half * BLOCK, BLOCK), CHIPS * BLOCK), :]
+    swap = pltpu.make_async_remote_copy(
+        src_ref=kind, dst_ref=kind, send_sem=send_sems.at[5], recv_sem=recv_sems.at[5, 0],
+        device_id=partner, device_id_type=LOGICAL,
+    )
+    swap.start()
+
+    def split_half(first):
+        for sub in range(BLOCK):
+            rows = pl.ds(first * BLOCK + sub, CHIPS, stride=BLOCK)
+            high, low = split_pair(masked_recv[rows, :])
+            lanes = slice(sub * 128, sub * 128 + 128)
+            masked_split[pl.ds(pl.multiple_of(first, CHIPS), CHIPS), lanes] = high
+            masked_split[pl.ds(pl.multiple_of(first, CHIPS) + DEVICES, CHIPS), lanes] = low
+
+    split_half(my_half)
+    swap.wait()
+    split_half(CHIPS - my_half)
 
     def strided(team, sub):
-        return pl.ds(team * (TEAM * 8) + sub, TEAM, stride=8)
+        return pl.ds(team * (TEAM * BLOCK) + sub, TEAM, stride=BLOCK)
 
     def correlate(stage, count):
         team = team_before(stage)
         drain(applied_recv, recv_sems.at[1, team], count)
-        parts = [split_pair(applied_recv[strided(team, sub), :]) for sub in range(8)]
+        parts = [split_pair(applied_recv[strided(team, sub), :]) for sub in range(BLOCK)]
         left = jnp.concatenate(
             [jnp.concatenate([part[which] for part in parts], axis=1) for which in range(2)], axis=0
         )
@@ -573,7 +597,7 @@
         drain(matrix, recv_sems.at[3, team], count)
         high, low = split_pair(matrix[pl.ds(team * TEAM, TEAM), 0, :])
         table = jnp.concatenate([high, high, low], axis=1)
-        for sub in range(0, 8, 2):
+        for sub in range(0, BLOCK, 2):
             lanes = slice(sub * 128, sub * 128 + 256)
             projected = dot32(
                 table,
@@ -602,7 +626,7 @@
     field = pltpu.VMEM(FIELD, F32)
     pitched = pltpu.VMEM(PITCHED, F32)
     tiles = pltpu.VMEM(TILES, F32)
-    rows = pltpu.VMEM((DEVICES, 1, 128), F32)
+    rows = pltpu.VMEM((CHIPS, 1, 128), F32)
     return pl.pallas_call(
         gradient_kernel,
         out_shape=(jax.ShapeDtypeStruct(TILES, F32), jax.ShapeDtypeStruct(FIELD, F32)),
@@ -610,12 +634,12 @@
         out_specs=in_vmem(1) + anywhere(1),
         scratch_shapes=[
             field, field, field, pitched, pitched, pitched, pitched,
-            tiles, tiles, tiles, tiles, tiles,
-            pltpu.VMEM((2 * DEVICES, 8 * 128), BF16),
+            tiles, pltpu.VMEM((2 * TILES[0], 128), F32), tiles, tiles, tiles,
+            pltpu.VMEM((2 * DEVICES, BLOCK * 128), BF16),
             rows, rows, pltpu.VMEM((1, 1, 128), F32), rows,
             pltpu.SemaphoreType.DMA((3,)),
-            pltpu.SemaphoreType.DMA((5,)),
-            pltpu.SemaphoreType.DMA((5, TEAMS)),
+            pltpu.SemaphoreType.DMA((6,)),
+            pltpu.SemaphoreType.DMA((6, TEAMS)),
         ],
         compiler_params=pltpu.CompilerParams(
             collective_id=0, has_side_effects=True, vmem_limit_bytes=VMEM_LIMIT

time: 61.9 us -> 54.2 us (0.88); the launches traced: 60.6 us -> 53.9 us
  Pallas kernels: 60 us -> 53.2 us
    pallas_call x1, Pallas kernels: 10 us -> 6.32 us  [precondition(): pl.pallas_call(precondition_kernel, out_shape=(shape, shape), in_specs=an...]
    pallas_call x1, Pallas kernels: 50 us -> 46.9 us  [gradient_fields(): pl.pallas_call(gradient_kernel, out_shape=(jax.ShapeDtypeStruct(TILES, F3...]
where the time goes in v4:
time: 54.2 us; the launch traced here: 53.9 us
  Pallas kernels  53.2 us (98%)
  between operations  0.64 us (1%)
    pallas_call x1, Pallas kernels, gradient_fields(): pl.pallas_call(gradient_kernel, out_shape=(jax.ShapeDtypeStruct(TILES, F3...  46.9 us
    pallas_call x1, Pallas kernels, precondition(): pl.pallas_call(precondition_kernel, out_shape=(shape, shape), in_specs=an...  6.32 us

profile of v4, /device:TPU:0, one launch (start us, length us, event | category | flops | bytes accessed | tf_op | source)
XLA Modules:
  0.0 53.9 jit_solution(17388074806407456628)
XLA Ops:
  0.6 46.9 %gradient.1 = (f32[1024,128]{1,0:T(8,128)}, f32[2048,128]{1,0:T(8,128)}) custom-call(f32[1,64,4096]{2,1,0:T(8,128)} %wave.1, f32[64,4096]{1,0:T(8,128)} %potential_hbm.1, s32[2,4096]{1,0:T(2,128)} %runs.1, bf16[384,256]{1,0:T(8,128)(2,1)} %constant.24.clone.lanes_kf, bf16[64,192]{1,0:T(8,128)(2,1)} %constant.25.clone.rows_k, ...), custom_call_target="tpu_custom_call" | custom-call | tf_op jit(solution)/shard_map/gradient/pallas_call | solution.py:630
  47.6 6.3 %precondition.1 = (f32[1,64,4096]{2,1,0:T(8,128)}, f32[1,64,4096]{2,1,0:T(8,128)}) custom-call(f32[1024,128]{1,0:T(8,128)} %get-tuple-element.4.tiles_hbm, f32[2048,128]{1,0:T(8,128)} %get-tuple-element.5.region_hbm, bf16[256,256]{1,0:T(8,128)(2,1)} %constant.32.clone.lanes_q, bf16[64,192]{1,0:T(8,128)(2,1)} %constant.33.clone.rows_q, ...), custom_call_target="tpu_custom_call" | custom-call | tf_op jit(solution)/shard_map/precondition/pallas_call | solution.py:390

commit v5 on v4

--- a/solution.py
+++ b/solution.py
@@ -306,9 +306,16 @@
     lax.fori_loop(0, count, step, 0, unroll=unroll)
 
 
+def copies_of(sources, targets, sems):
+    return [
+        pltpu.make_async_copy(source, target, sems.at[place])
+        for place, (source, target) in enumerate(zip(sources, targets))
+    ]
+
+
 def precondition_kernel(
-    tiles_hbm, region_hbm, lanes_q, rows_q, columns_q, symbol_hbm, gradient_out, preconditioned_out,
-    tiles, region, gradient, work, symbol, load_sems, sems,
+    tiles_hbm, region_hbm, lanes_hbm, rows_hbm, columns_hbm, symbol_hbm, gradient_out, preconditioned_out,
+    lanes_q, rows_q, columns_q, symbol, tiles, region, gradient, work, table_sems, load_sems, sems,
 ):
     def fetch(group):
         rows = pl.ds(group * GROUP * GRID, GROUP * GRID)
@@ -318,11 +325,20 @@
             pltpu.make_async_copy(region_hbm.at[planes], region.at[planes], load_sems.at[1, group]),
         )
 
-    for group in range(GROUPS):
+    tables = copies_of(
+        (lanes_hbm, rows_hbm, columns_hbm, symbol_hbm), (lanes_q, rows_q, columns_q, symbol), table_sems
+    )
+    for copy in fetch(0):
+        copy.start()
+    for copy in tables[:2]:
+        copy.start()
+    for group in range(1, GROUPS):
         for copy in fetch(group):
             copy.start()
-    symbol_copy = pltpu.make_async_copy(symbol_hbm, symbol, sems.at[0])
-    symbol_copy.start()
+    for copy in tables[2:]:
+        copy.start()
+    for copy in tables[:2]:
+        copy.wait()
 
     def put(buffer, target, pair, sem):
         for plane in (2 * pair, 2 * pair + 1):
@@ -346,7 +362,8 @@
             put_both_planes(work, pair, along_rows(rows_q[...], value))
 
     loop(GROUPS, head, GROUPS)
-    symbol_copy.wait()
+    for copy in tables[2:]:
+        copy.wait()
 
     def middle(step):
         first = 4 * step
@@ -387,26 +404,24 @@
     field = pltpu.VMEM(FIELD, F32)
     pitched = pltpu.VMEM(PITCHED, F32)
     shape = jax.ShapeDtypeStruct((1, GRID, GRID * GRID), F32)
+    tables = [
+        jnp.asarray(table)
+        for table in (lanes_table(modes), rows_table(modes), columns_table(modes), chebyshev_symbol())
+    ]
     return pl.pallas_call(
         precondition_kernel,
         out_shape=(shape, shape),
-        in_specs=anywhere(2) + in_vmem(3) + anywhere(1),
+        in_specs=anywhere(2 + len(tables)),
         out_specs=anywhere(2),
-        scratch_shapes=[
-            pltpu.VMEM(TILES, F32), field, field, pitched, pltpu.VMEM((GRID // 4 * GRID, 256), F32),
+        scratch_shapes=[pltpu.VMEM(table.shape, table.dtype) for table in tables] + [
+            pltpu.VMEM(TILES, F32), field, field, pitched,
+            pltpu.SemaphoreType.DMA((len(tables),)),
             pltpu.SemaphoreType.DMA((2, GROUPS)),
             pltpu.SemaphoreType.DMA((3,)),
         ],
         compiler_params=pltpu.CompilerParams(vmem_limit_bytes=VMEM_LIMIT),
         name="precondition",
-    )(
-        tiles,
-        region,
-        jnp.asarray(lanes_table(modes)),
-        jnp.asarray(rows_table(modes)),
-        jnp.asarray(columns_table(modes)),
-        jnp.asarray(chebyshev_symbol()),
-    )
+    )(tiles, region, *tables)
 
 
 def hamiltonian_tables():
@@ -429,6 +444,10 @@
     return pl.ds(pl.multiple_of(index * BLOCK, BLOCK), BLOCK)
 
 
+def spaced(index):
+    return pl.ds(index * SPACE, BLOCK)
+
+
 def row_of(index):
     return pl.ds(index, 1)
 
@@ -437,20 +456,25 @@
 CHIPS = DEVICES // 2
 TEAM = CHIPS // TEAMS
 BLOCK = 16
+SPACE = BLOCK + 1
 LOGICAL = pl.DeviceIdType.LOGICAL
 SEND_UNROLL = 8
+EARLY = 2
 
 
 def gradient_kernel(
-    wave, potential_hbm, runs, lanes_kf, rows_k, rows_f, columns_k, columns_f, columns_b, rows_b, lanes_b,
+    wave, potential_hbm,
+    runs_hbm, kf_hbm, k_hbm, f_hbm, ck_hbm, cf_hbm, cb_hbm, b_hbm, lb_hbm,
     gradient_tiles, region_out,
+    runs, lanes_kf, rows_k, rows_f, columns_k, columns_f, columns_b, rows_b, lanes_b,
     waves, staged, region, masked, kinetic, forward, potential,
     masked_send, masked_recv, applied_send, applied_recv, back_send,
     masked_split, partial, gathered, row, matrix,
-    load_sems, send_sems, recv_sems,
+    table_sems, load_sems, send_sems, recv_sems,
 ):
     chip = lax.axis_index("orb")
     core = lax.axis_index("pair")
+    device = chip * 2 + core
     my_team = jnp.bitwise_and(lax.shift_right_logical(chip, 1), 2) + jnp.bitwise_and(chip, 1)
     my_seat = jnp.bitwise_and(lax.shift_right_logical(chip, 2), 14) + jnp.bitwise_and(
         lax.shift_right_logical(chip, 1), 1
@@ -460,75 +484,87 @@
     barrier = pltpu.get_barrier_semaphore()
 
     def greet(step):
-        peer = jnp.bitwise_and(chip + (step + 1), CHIPS - 1) * 2 + core
+        peer = jnp.bitwise_xor(device, 2 * (CHIPS - 1 - step))
         pl.semaphore_signal(barrier, inc=1, device_id=peer, device_id_type=LOGICAL)
 
+    tables = copies_of(
+        (runs_hbm, kf_hbm, k_hbm, f_hbm, ck_hbm, cf_hbm, cb_hbm, b_hbm, lb_hbm),
+        (runs, lanes_kf, rows_k, rows_f, columns_k, columns_f, columns_b, rows_b, lanes_b),
+        table_sems,
+    )
+    tables[0].start()
     load_planes(wave.at[0], waves, load_sems.at[0])
+    for copy in tables[1:]:
+        copy.start()
     loop(CHIPS - 1, greet, SEND_UNROLL)
-    partner = chip * 2 + (1 - core)
+    partner = jnp.bitwise_xor(device, 1)
     pl.semaphore_signal(barrier, inc=1, device_id=partner, device_id_type=LOGICAL)
     load_planes(potential_hbm, staged, load_sems.at[1])
+    tables[0].wait()
     bounds = run_bounds(runs[...])
     wait_planes(waves, load_sems.at[0])
 
-    def team_after(stage):
-        return jnp.bitwise_and(my_team + (stage + 1), TEAMS - 1)
-
-    def team_before(stage):
-        return jnp.bitwise_and(my_team + (TEAMS - 1 - stage), TEAMS - 1)
-
-    def send_team(source, target, phase, team, count, source_at, target_at, signal):
-        base = jnp.bitwise_and(team, 2) * 4 + jnp.bitwise_and(team, 1) * 2 + core
+    def team_at(stage):
+        return jnp.bitwise_xor(my_team, stage)
+
+    def send_team(source, target, phase, stage, source_at, target_at, signal):
+        apart = (stage & 2) * 4 + (stage & 1) * 2
 
         def send(step):
-            seat = jnp.bitwise_and(my_seat + (step + 1), TEAM - 1)
+            seat = TEAM - 1 - step
             pltpu.make_async_remote_copy(
-                src_ref=source.at[source_at(team * TEAM + seat)],
+                src_ref=source.at[source_at(jnp.bitwise_xor(me, stage * TEAM + seat))],
                 dst_ref=target.at[target_at(me)],
                 send_sem=send_sems.at[phase],
                 recv_sem=recv_sems.at[phase, signal],
-                device_id=jnp.bitwise_and(seat, 14) * 8 + jnp.bitwise_and(seat, 1) * 4 + base,
+                device_id=jnp.bitwise_xor(
+                    device, jnp.bitwise_and(seat, 14) * 8 + jnp.bitwise_and(seat, 1) * 4 + apart
+                ),
                 device_id_type=LOGICAL,
             ).start()
 
-        loop(count, send, SEND_UNROLL)
+        loop(size_of(stage), send, size_of(stage))
 
     def size_of(stage):
-        return TEAM if stage < TEAMS - 1 else TEAM - 1
+        return TEAM if stage else TEAM - 1
 
     def scatter(source, target, phase, source_at, target_at, signal=0):
         for stage in range(TEAMS):
-            send_team(
-                source, target, phase, team_after(stage), size_of(stage), source_at, target_at, signal
-            )
+            send_team(source, target, phase, stage, source_at, target_at, signal)
 
     def drain(buffer, sem, count=CHIPS - 1):
         whole = buffer.at[pl.ds(0, buffer.shape[0] * count // CHIPS)]
         pltpu.make_async_copy(whole, whole, sem).wait()
 
+    def mask_pair(pair):
+        mask = region_pair(bounds, pair)
+        put_both_planes(region, pair, mask, block_of)
+        value = both_planes(waves, pair, block_of) * mask
+        put_both_planes(masked, pair, value)
+        masked_send[block_of(pair), :] = fold_pair(value)
+
     def head(group):
-        values = []
-        for pair in pairs_of(group):
-            mask = region_pair(bounds, pair)
-            put_both_planes(region, pair, mask, block_of)
-            value = both_planes(waves, pair, block_of) * mask
-            put_both_planes(masked, pair, value)
-            masked_send[block_of(pair), :] = fold_pair(value)
-            values.append(value)
+        values = [both_planes(masked, pair) for pair in pairs_of(group)]
         hamiltonian_head(kinetic, forward, (lanes_kf, rows_k, rows_f), group, values)
 
-    loop(GROUPS, head, GROUPS)
+    loop(PLANES // 2, mask_pair, PLANES // 2)
     region_copy = pltpu.make_async_copy(region, region_out, load_sems.at[2])
     region_copy.start()
+    for copy in tables[1:]:
+        copy.wait()
+    for group in range(EARLY):
+        head(group)
+    pl.semaphore_wait(barrier, CHIPS)
+    scatter(masked_send, masked_recv, 0, tile_of, lambda label: spaced(my_half + label))
+    masked_recv[spaced(my_half + me), :] = masked_send[tile_of(me), :]
+    for group in range(EARLY, GROUPS):
+        head(group)
     wait_planes(staged, load_sems.at[1])
 
     def pitch(pair):
         put_both_planes(potential, pair, both_planes(staged, pair, block_of))
 
     loop(PLANES // 2, pitch, 4)
-    pl.semaphore_wait(barrier, CHIPS)
-    scatter(masked_send, masked_recv, 0, tile_of, lambda label: tile_of(my_half + label))
-    masked_recv[tile_of(my_half + me), :] = masked_send[tile_of(me), :]
 
     def middle(step):
         hamiltonian_middle(
@@ -537,18 +573,18 @@
 
     loop(GRID // 4, middle, MIDDLE_UNROLL)
 
-    def tail(stage, count):
-        team = team_after(stage)
+    def tail(stage):
+        team = team_at(stage)
         values = hamiltonian_tail(kinetic, forward, (rows_b, lanes_b), team)
         for pair, value in zip(pairs_of(team), values):
             applied_send[block_of(pair), :] = fold_pair(value * both_planes(region, pair, block_of))
-        send_team(applied_send, applied_recv, 1, team, count, tile_of, tile_of, my_team)
-
-    loop(TEAMS - 1, lambda stage: tail(stage, TEAM))
-    tail(TEAMS - 1, TEAM - 1)
-    applied_recv[tile_of(me), :] = applied_send[tile_of(me), :]
-    drain(masked_recv.at[pl.ds(0, CHIPS * BLOCK)], recv_sems.at[0, 0])
-    kind = masked_recv.at[pl.ds(pl.multiple_of(my_half * BLOCK, BLOCK), CHIPS * BLOCK), :]
+        send_team(applied_send, applied_recv, 1, stage, tile_of, spaced, my_team)
+
+    for stage in range(TEAMS):
+        tail(stage)
+    applied_recv[spaced(me), :] = applied_send[tile_of(me), :]
+    drain(masked_send, recv_sems.at[0, 0])
+    kind = masked_recv.at[pl.ds(pl.multiple_of(my_half * SPACE, 8), CHIPS * SPACE), :]
     swap = pltpu.make_async_remote_copy(
         src_ref=kind, dst_ref=kind, send_sem=send_sems.at[5], recv_sem=recv_sems.at[5, 0],
         device_id=partner, device_id_type=LOGICAL,
@@ -557,7 +593,7 @@
 
     def split_half(first):
         for sub in range(BLOCK):
-            rows = pl.ds(first * BLOCK + sub, CHIPS, stride=BLOCK)
+            rows = pl.ds(first * SPACE + sub, CHIPS, stride=SPACE)
             high, low = split_pair(masked_recv[rows, :])
             lanes = slice(sub * 128, sub * 128 + 128)
             masked_split[pl.ds(pl.multiple_of(first, CHIPS), CHIPS), lanes] = high
@@ -568,11 +604,11 @@
     split_half(CHIPS - my_half)
 
     def strided(team, sub):
-        return pl.ds(team * (TEAM * BLOCK) + sub, TEAM, stride=BLOCK)
-
-    def correlate(stage, count):
-        team = team_before(stage)
-        drain(applied_recv, recv_sems.at[1, team], count)
+        return pl.ds(team * (TEAM * SPACE) + sub, TEAM, stride=SPACE)
+
+    def correlate(stage):
+        team = team_at(stage)
+        drain(applied_send, recv_sems.at[1, team], size_of(stage))
         parts = [split_pair(applied_recv[strided(team, sub), :]) for sub in range(BLOCK)]
         left = jnp.concatenate(
             [jnp.concatenate([part[which] for part in parts], axis=1) for which in range(2)], axis=0
@@ -582,19 +618,19 @@
         )
         rows = total[:TEAM, :DEVICES] + (total[:TEAM, DEVICES:] + total[TEAM:, :DEVICES])
         partial[pl.ds(team * TEAM, TEAM), 0, :] = rows
-        send_team(partial, gathered, 2, team, count, row_of, row_of, 0)
-
-    loop(TEAMS - 1, lambda stage: correlate(stage, TEAM))
-    correlate(TEAMS - 1, TEAM - 1)
+        send_team(partial, gathered, 2, stage, row_of, row_of, 0)
+
+    for stage in range(TEAMS):
+        correlate(stage)
     gathered[row_of(me)] = partial[row_of(me)]
     drain(gathered, recv_sems.at[2, 0])
     row[...] = jnp.sum(gathered[...], axis=0, keepdims=True) * (1.0 / CELLS)
     scatter(row, matrix, 3, lambda peer: pl.ds(0, 1), row_of, my_team)
     matrix[row_of(me)] = row[...]
 
-    def project(stage, count):
-        team = team_before(stage)
-        drain(matrix, recv_sems.at[3, team], count)
+    def project(stage):
+        team = team_at(stage)
+        drain(matrix, recv_sems.at[3, team], size_of(stage))
         high, low = split_pair(matrix[pl.ds(team * TEAM, TEAM), 0, :])
         table = jnp.concatenate([high, high, low], axis=1)
         for sub in range(0, BLOCK, 2):
@@ -608,36 +644,41 @@
                 back_send[rows, :] = (
                     applied_recv[rows, :] - projected[:, shift * 128 : shift * 128 + 128]
                 )
-        send_team(back_send, gradient_tiles, 4, team, count, tile_of, tile_of, 0)
-
-    loop(TEAMS - 1, lambda stage: project(stage, TEAM))
-    project(TEAMS - 1, TEAM - 1)
-    gradient_tiles[tile_of(me), :] = back_send[tile_of(me), :]
+        send_team(back_send, gradient_tiles, 4, stage, spaced, tile_of, 0)
+
+    for stage in range(TEAMS):
+        project(stage)
+    own = pltpu.make_async_copy(back_send.at[spaced(me)], gradient_tiles.at[tile_of(me)], load_sems.at[3])
+    own.start()
     region_copy.wait()
+    own.wait()
     drain(masked_send, send_sems.at[0])
     drain(applied_send, send_sems.at[1])
     drain(partial, send_sems.at[2])
     drain(matrix, send_sems.at[3])
     drain(gradient_tiles, recv_sems.at[4, 0])
-    drain(back_send, send_sems.at[4])
+    drain(gradient_tiles, send_sems.at[4])
 
 
 def gradient_fields(wavefunctions, potential, line_runs):
     field = pltpu.VMEM(FIELD, F32)
     pitched = pltpu.VMEM(PITCHED, F32)
     tiles = pltpu.VMEM(TILES, F32)
+    spaces = pltpu.VMEM((CHIPS * SPACE, 128), F32)
     rows = pltpu.VMEM((CHIPS, 1, 128), F32)
+    tables = [line_runs, *hamiltonian_tables()]
     return pl.pallas_call(
         gradient_kernel,
         out_shape=(jax.ShapeDtypeStruct(TILES, F32), jax.ShapeDtypeStruct(FIELD, F32)),
-        in_specs=anywhere(2) + in_vmem(9),
-        out_specs=in_vmem(1) + anywhere(1),
-        scratch_shapes=[
+        in_specs=anywhere(2 + len(tables)),
+        out_specs=anywhere(2),
+        scratch_shapes=[pltpu.VMEM(table.shape, table.dtype) for table in tables] + [
             field, field, field, pitched, pitched, pitched, pitched,
-            tiles, pltpu.VMEM((2 * TILES[0], 128), F32), tiles, tiles, tiles,
+            tiles, pltpu.VMEM((DEVICES * SPACE, 128), F32), tiles, spaces, spaces,
             pltpu.VMEM((2 * DEVICES, BLOCK * 128), BF16),
             rows, rows, pltpu.VMEM((1, 1, 128), F32), rows,
-            pltpu.SemaphoreType.DMA((3,)),
+            pltpu.SemaphoreType.DMA((len(tables),)),
+            pltpu.SemaphoreType.DMA((4,)),
             pltpu.SemaphoreType.DMA((6,)),
             pltpu.SemaphoreType.DMA((6, TEAMS)),
         ],
@@ -645,7 +686,7 @@
             collective_id=0, has_side_effects=True, vmem_limit_bytes=VMEM_LIMIT
         ),
         name="gradient",
-    )(wavefunctions, potential, line_runs, *hamiltonian_tables())
+    )(wavefunctions, potential, *tables)
 
 
 def on_device(wavefunctions, potential, line_runs):

time: 54.2 us -> 51.2 us (0.945)
  Pallas kernels: 53.2 us -> 50.3 us
    pallas_call x1, Pallas kernels: 46.9 us -> 44.7 us  [gradient_fields(): pl.pallas_call(gradient_kernel, out_shape=(jax.ShapeDtypeStruct(TILES, F3...]
    pallas_call x1, Pallas kernels: 6.32 us -> 5.61 us  [precondition(): pl.pallas_call(precondition_kernel, out_shape=(shape, shape), in_specs=an...]
where the time goes in v5:
time: 51.2 us; the launch traced here: 51.1 us
  Pallas kernels  50.3 us (98%)
  between operations  0.8 us (2%)
    pallas_call x1, Pallas kernels, gradient_fields(): pl.pallas_call(gradient_kernel, out_shape=(jax.ShapeDtypeStruct(TILES, F3...  44.7 us
    pallas_call x1, Pallas kernels, precondition(): pl.pallas_call(precondition_kernel, out_shape=(shape, shape), in_specs=an...  5.61 us

profile of v5, /device:TPU:0, one launch (start us, length us, event | category | flops | bytes accessed | tf_op | source)
XLA Modules:
  0.0 51.1 jit_solution(7267073826056854597)
XLA Ops:
  0.6 44.7 %gradient.1 = (f32[1024,128]{1,0:T(8,128)}, f32[2048,128]{1,0:T(8,128)}) custom-call(f32[1,64,4096]{2,1,0:T(8,128)} %wave.1, f32[64,4096]{1,0:T(8,128)} %potential_hbm.1, s32[2,4096]{1,0:T(2,128)} %runs_hbm.1, bf16[384,256]{1,0:T(8,128)(2,1)} %constant.24.clone.kf_hbm, bf16[64,192]{1,0:T(8,128)(2,1)} %constant.25.clone.k_hbm, ...), custom_call_target="tpu_custom_call" | custom-call | tf_op jit(solution)/shard_map/gradient/pallas_call | solution.py:670
  45.3 5.6 %precondition.1 = (f32[1,64,4096]{2,1,0:T(8,128)}, f32[1,64,4096]{2,1,0:T(8,128)}) custom-call(f32[1024,128]{1,0:T(8,128)} %get-tuple-element.4.tiles_hbm, f32[2048,128]{1,0:T(8,128)} %get-tuple-element.5.region_hbm, bf16[256,256]{1,0:T(8,128)(2,1)} %constant.32.clone.lanes_hbm, bf16[64,192]{1,0:T(8,128)(2,1)} %constant.33.clone.rows_hbm, ...), custom_call_target="tpu_custom_call" | custom-call | tf_op jit(solution)/shard_map/precondition/pallas_call | solution.py:411
